TPU v7x, 32 devices: a whole 2x2x4 slice. The times are simulated.
32 devices in a mesh: seq: 8 (over z, x), head: 4 (over y, core).
Axes of the slice: x: 2, y: 2, z: 4, core: 2. Of those that a mesh axis runs over, the one named last changes fastest.
Arguments:
- context: bfloat16 [16384, 2048], P('seq'), may hold values from -64 to 64
- wq_cross: bfloat16 [2048, 2048], P(None, 'head'), may hold values from -4 to 4
- wk_cross: bfloat16 [2048, 2048], P(None, 'head'), may hold values from -4 to 4
- wv_cross: bfloat16 [2048, 2048], P(None, 'head'), may hold values from -0.125 to 0.125
- wo_cross: bfloat16 [2048, 2048], P('head'), may hold values from -0.125 to 0.125
- wq_latent: bfloat16 [2048, 2048], P(None, 'head'), may hold values from -4 to 4
- wk_latent: bfloat16 [2048, 2048], P(None, 'head'), may hold values from -4 to 4
- wv_latent: bfloat16 [2048, 2048], P(None, 'head'), may hold values from -0.125 to 0.125
- wo_latent: bfloat16 [2048, 2048], P('head'), may hold values from -0.125 to 0.125
- cross_keep: int32 [16, 2048, 2048], P('head', None, 'seq'), may hold values from 0 to 255, as said below
- latent_keep: int32 [16, 2048, 128], P('head'), may hold values from 0 to 65535, as said below
- residual_keep: int32 [2, 2048, 128], replicated, may hold values from 0 to 65535, as said below
Outputs:
- latents_out: bfloat16 [2048, 2048], P('seq', 'head')
Inputs may be any that keep to these rules, and one draw needn't show every extreme that they name: `cross_keep`: each of the 8 low bits of a word is one keep flag, laid out as the steps say. `latent_keep`: each of the 16 low bits of a word is one keep flag, laid out as the steps say. `residual_keep`: each of the 16 low bits of a word is one keep flag, laid out as the steps say.
All inputs are finite; a program needn't handle non-finite values.
Results may differ from a plain program's by a relative error of at most 0.015.
Values may be sent and summed in bfloat16 or wider, within the bound.
A program may use at most 128 MiB of HBM per device.

v0:
```python
import math

import jax
import jax.numpy as jnp
from jax import lax
from jax.sharding import PartitionSpec as P

keep_scale = 8.0 / 7.0
masked = -1e30


def from_root(value, axis, source):
    kept = jnp.where(lax.axis_index(axis) == source, value, 0).astype(value.dtype)
    return lax.psum(kept, axis)


def unpack_bits(packed_words, word_bits):
    shifts = jnp.arange(word_bits, dtype=jnp.int32)
    bit_table = jnp.bitwise_and(jnp.right_shift(packed_words[..., None, :], shifts[:, None]), 1)
    return bit_table.reshape(packed_words.shape[:-1] + (word_bits * packed_words.shape[-1],))


def rms_rows(matrix):
    wide_rows = matrix.astype(jnp.float32)
    mean_square = jnp.mean(wide_rows * wide_rows, axis=-1, keepdims=True)
    return (wide_rows * lax.rsqrt(mean_square + 1e-06)).astype(jnp.bfloat16)


def per_device(
    context,
    wq_cross,
    wk_cross,
    wv_cross,
    wo_cross,
    wq_latent,
    wk_latent,
    wv_latent,
    wo_latent,
    cross_keep,
    latent_keep,
    residual_keep,
):
    seq_count = lax.axis_size("seq")
    seq_index = lax.axis_index("seq")
    head_index = lax.axis_index("head")
    tok_rows, model_width = context.shape
    head_local = cross_keep.shape[0]
    latent_count = cross_keep.shape[1]
    head_dim = wq_cross.shape[1] // head_local
    query_width = head_local * head_dim
    columns = model_width // lax.axis_size("head")
    local_rows = latent_count // seq_count
    score_scale = 1.0 / math.sqrt(head_dim)
    normed = rms_rows(context)
    key_rows = jnp.dot(normed, wk_cross, preferred_element_type=jnp.float32).astype(jnp.bfloat16)
    value_rows = jnp.dot(normed, wv_cross, preferred_element_type=jnp.float32).astype(jnp.bfloat16)
    own_queries = jnp.dot(normed, wq_cross, preferred_element_type=jnp.float32).astype(jnp.bfloat16)
    own_columns = lax.dynamic_slice_in_dim(context, head_index * columns, columns, 1)
    outgoing_rows = jnp.concatenate([own_queries, own_columns], axis=1)
    arrived_rows = from_root(outgoing_rows, "seq", seq_count - 1)
    queries = arrived_rows[:, :query_width]
    latent_context = arrived_rows[:, query_width:]
    first_latent = (seq_count - 1) * tok_rows
    block_rows = min(512, latent_count)
    block_count = latent_count // block_rows
    query_blocks = queries.reshape(block_count, block_rows, head_local, head_dim)
    mask_blocks = cross_keep.reshape(head_local, block_count, block_rows, -1).transpose(1, 0, 2, 3)
    key_heads = key_rows.reshape(tok_rows, head_local, head_dim)
    value_heads = value_rows.reshape(tok_rows, head_local, head_dim)
    key_pos = seq_index * tok_rows + jnp.arange(tok_rows, dtype=jnp.int32)

    def cross_block(block_items):
        query_block, mask_block, number = block_items
        scores = (
            jnp.einsum("qhd,khd->hqk", query_block, key_heads, preferred_element_type=jnp.float32)
            * score_scale
        )
        query_pos = first_latent + number * block_rows + jnp.arange(block_rows, dtype=jnp.int32)
        allowed = key_pos[None, None, :] <= query_pos[None, :, None]
        scores = jnp.where(allowed, scores, masked)
        row_top = jnp.max(scores, axis=-1)
        exponent = jnp.where(allowed, jnp.exp(scores - row_top[..., None]), 0.0)
        row_sum = jnp.sum(exponent, axis=-1)
        keep_flags = unpack_bits(mask_block, 8).astype(jnp.float32)
        weights = (exponent * keep_flags * keep_scale).astype(jnp.bfloat16)
        summed = jnp.einsum(
            "hqk,khd->hqd", weights, value_heads, preferred_element_type=jnp.float32
        )
        return (summed, row_top, row_sum)

    summed, row_top, row_sum = lax.map(
        cross_block, (query_blocks, mask_blocks, jnp.arange(block_count, dtype=jnp.int32))
    )
    summed = summed.transpose(1, 0, 2, 3).reshape(head_local, latent_count, head_dim)
    row_top = row_top.transpose(1, 0, 2).reshape(head_local, latent_count)
    row_sum = row_sum.transpose(1, 0, 2).reshape(head_local, latent_count)
    first_row = seq_index * local_rows
    row_peak = lax.pmax(row_top, "seq")
    factor = jnp.exp(row_top - row_peak)
    numerator, denominator = (
        lax.psum_scatter(
            (summed * factor[..., None]).astype(jnp.bfloat16),
            "seq",
            scatter_dimension=1,
            tiled=True,
        ).astype(jnp.float32),
        lax.psum_scatter(
            (row_sum * factor).astype(jnp.bfloat16), "seq", scatter_dimension=1, tiled=True
        ).astype(jnp.float32),
    )
    attended_heads = numerator / denominator[..., None]
    attended = (
        attended_heads.transpose(1, 0, 2)
        .reshape(local_rows, head_local * head_dim)
        .astype(jnp.bfloat16)
    )
    inputs = lax.dynamic_slice_in_dim(latent_context, first_row, local_rows, 0).astype(jnp.float32)
    residual_rows = lax.dynamic_slice_in_dim(residual_keep, first_row, local_rows, 1)
    residual_mask = lax.dynamic_slice_in_dim(
        unpack_bits(residual_rows, 16), head_index * columns, columns, 2
    ).astype(jnp.float32)
    branch = jnp.dot(attended, wo_cross, preferred_element_type=jnp.float32)
    branch = lax.psum_scatter(
        branch.astype(jnp.bfloat16), "head", scatter_dimension=1, tiled=True
    ).astype(jnp.float32)
    latents = (inputs + residual_mask[0] * keep_scale * branch).astype(jnp.bfloat16)
    wide_latents = latents.astype(jnp.float32)
    squares = lax.psum(jnp.sum(wide_latents * wide_latents, axis=-1), "head")
    normed_columns = (wide_latents * lax.rsqrt(squares / model_width + 1e-06)[:, None]).astype(
        jnp.bfloat16
    )
    normed_latents = lax.all_gather(normed_columns, "head", axis=1, tiled=True)
    latent_queries = jnp.dot(normed_latents, wq_latent, preferred_element_type=jnp.float32).astype(
        jnp.bfloat16
    )
    latent_keys = jnp.dot(normed_latents, wk_latent, preferred_element_type=jnp.float32).astype(
        jnp.bfloat16
    )
    latent_values = jnp.dot(normed_latents, wv_latent, preferred_element_type=jnp.float32).astype(
        jnp.bfloat16
    )
    my_index = first_row + jnp.arange(local_rows, dtype=jnp.int32)
    latent_words = lax.dynamic_slice_in_dim(latent_keep, first_row, local_rows, 1)
    latent_mask = unpack_bits(latent_words, 16).astype(jnp.float32)
    query_heads = latent_queries.reshape(local_rows, head_local, head_dim)
    initial = (
        jnp.zeros((head_local, local_rows, head_dim), jnp.float32),
        jnp.full((head_local, local_rows), masked, jnp.float32),
        jnp.zeros((head_local, local_rows), jnp.float32),
    )
    key_piece = lax.all_gather(latent_keys, "seq", axis=0, tiled=True)
    value_piece = lax.all_gather(latent_values, "seq", axis=0, tiled=True)
    piece_rows = key_piece.shape[0]
    key_index = jnp.arange(piece_rows, dtype=jnp.int32)

    def update(current):
        weighted, old_top, old_sum = current
        scores = (
            jnp.einsum(
                "qhd,khd->hqk",
                query_heads,
                key_piece.reshape(piece_rows, head_local, head_dim),
                preferred_element_type=jnp.float32,
            )
            * score_scale
        )
        allowed = key_index[None, None, :] <= my_index[None, :, None]
        scores = jnp.where(allowed, scores, masked)
        new_top = jnp.maximum(old_top, jnp.max(scores, axis=-1))
        exponent = jnp.where(allowed, jnp.exp(scores - new_top[..., None]), 0.0)
        keep_flags = jnp.take(latent_mask, key_index, axis=2)
        weights = (exponent * keep_flags * keep_scale).astype(jnp.bfloat16)
        added = jnp.einsum(
            "hqk,khd->hqd",
            weights,
            value_piece.reshape(piece_rows, head_local, head_dim),
            preferred_element_type=jnp.float32,
        )
        return (added, new_top, jnp.sum(exponent, axis=-1))

    needed = jnp.min(key_index) <= jnp.max(my_index)
    weighted, latent_top, latent_sum = lax.cond(needed, update, lambda current: current, initial)
    latent_attended = (
        (weighted / latent_sum[..., None])
        .transpose(1, 0, 2)
        .reshape(local_rows, head_local * head_dim)
        .astype(jnp.bfloat16)
    )
    latent_branch = jnp.dot(latent_attended, wo_latent, preferred_element_type=jnp.float32)
    latent_branch = lax.psum_scatter(
        latent_branch.astype(jnp.bfloat16), "head", scatter_dimension=1, tiled=True
    ).astype(jnp.float32)
    result = (wide_latents + residual_mask[1] * keep_scale * latent_branch).astype(jnp.bfloat16)
    return result


def solution(mesh):
    in_specs = (
        P("seq", None),
        P(None, "head"),
        P(None, "head"),
        P(None, "head"),
        P("head", None),
        P(None, "head"),
        P(None, "head"),
        P(None, "head"),
        P("head", None),
        P("head", None, "seq"),
        P("head", None, None),
        P(),
    )
    out_specs = P("seq", "head")
    return jax.shard_map(
        per_device, mesh=mesh, in_specs=in_specs, out_specs=out_specs, check_vma=False
    )
```

profile of v0, /device:TPU:11, one launch (start us, length us, event | category | flops | bytes accessed | tf_op | source)
XLA Modules:
  0.0 866.6 jit_solution(609139487656249483)
XLA Ops:
  55.9 132.2 %all-reduce.2.cloned.1.call-done = bf16[2048,1024]{0,1:T(8,128)(2,1)} async-done(((bf16[2048,1024]{0,1:T(8,128)(2,1)}), bf16[2048,1024]{0,1:T(8,128)(2,1)}) %all-reduce.2.cloned.1.call-update) | async-done | bytes 4194320 | tf_op jit(solution)/shard_map/psum | solution.py:14
  199.2 254.3 %while.15 = (s32[]{:T(128)}, f32[4,4,512,128]{3,2,0,1:T(8,128)}, f32[4,4,512]{2,1,0:T(4,128)S(1)}, f32[4,4,512]{2,1,0:T(4,128)S(1)}, s32[4]{0:T(128)S(1)}, /*ind...) while((s32[]{:T(128)}, f32[4,4,512,128]{3,2,0,1:T(8,128)}, ...), condition=%wide.region_5.6_spmd.clone, body=%wide.region_2.5_spmd.clone.sunk | while | flops 2224028160 | bytes 142201040 | solution.py:91
  208.4 18.0 %shift_right_arithmetic.116 = s32[4,512,2048]{2,1,0:T(8,128)} reshape(s32[4,512,8,256]{3,2,1,0:T(8,128)} %shift_right_arithmetic.115) | data formatting | bytes 33554432 | tf_op jit(solution)/shard_map/while/body/eval_jaxpr/shift_right_arithmetic | solution.py:19
  228.2 10.9 %fusion.86 = (f32[4,512]{1,0:T(4,128)S(1)}, f32[4,512,2048]{2,1,0:T(8,128)}) fusion(pred[512,2048]{1,0:T(8,128)(4,1)S(1)} %broadcast_compare_fusion.3, bf16[2048,4,128]{2,0,1:T(8,128)(2,1)} %get-tuple-element.276, bf16[4,512,4,128]{3,1,2,0:T(8,128)(2,1)} %get-tuple-element.275, s32[]{:T(128)S(6)} %copy.100), kind=kOutput, calls=%fused_computation.33.clone.1 | convolution fusion | flops 1086322688 | bytes 20455428 | tf_op jit(solution)/shard_map/while/body/eval_jaxpr/qhd,khd->hqk/dot_general | solution.py:75
  239.2 15.4 %fusion.87 = f32[4,4,512,128]{3,2,0,1:T(8,128)} fusion(f32[4,4,512,128]{3,2,0,1:T(8,128)} %get-tuple-element.258, s32[]{:T(128)S(6)} %copy.100, bf16[2048,4,128]{2,0,1:T(8,128)(2,1)S(1)} %copy-done.3, s32[4,512,2048]{2,1,0:T(8,128)} %shift_right_arithmetic.116, f32[4,512,2048]{2,1,0:T(8,128)} %get-tuple-element.240, s32[2048]{0:T(1024)S(1)} %bitcast.148, ...), kind=kOutput, calls=%fused_computation.40.clone.1 | convolution fusion | flops 1115684864 | bytes 37765124 | tf_op jit(solution)/shard_map/while/body/eval_jaxpr/hqk,khd->hqd/dot_general | solution.py:86
  271.9 18.0 %shift_right_arithmetic.116 = s32[4,512,2048]{2,1,0:T(8,128)} reshape(s32[4,512,8,256]{3,2,1,0:T(8,128)} %shift_right_arithmetic.115) | data formatting | bytes 33554432 | tf_op jit(solution)/shard_map/while/body/eval_jaxpr/shift_right_arithmetic | solution.py:19
  291.7 10.9 %fusion.86 = (f32[4,512]{1,0:T(4,128)S(1)}, f32[4,512,2048]{2,1,0:T(8,128)}) fusion(pred[512,2048]{1,0:T(8,128)(4,1)S(1)} %broadcast_compare_fusion.3, bf16[2048,4,128]{2,0,1:T(8,128)(2,1)} %get-tuple-element.276, bf16[4,512,4,128]{3,1,2,0:T(8,128)(2,1)} %get-tuple-element.275, s32[]{:T(128)S(6)} %copy.100), kind=kOutput, calls=%fused_computation.33.clone.1 | convolution fusion | flops 1086322688 | bytes 20455428 | tf_op jit(solution)/shard_map/while/body/eval_jaxpr/qhd,khd->hqk/dot_general | solution.py:75
  302.7 15.5 %fusion.87 = f32[4,4,512,128]{3,2,0,1:T(8,128)} fusion(f32[4,4,512,128]{3,2,0,1:T(8,128)} %get-tuple-element.258, s32[]{:T(128)S(6)} %copy.100, bf16[2048,4,128]{2,0,1:T(8,128)(2,1)S(1)} %copy-done.3, s32[4,512,2048]{2,1,0:T(8,128)} %shift_right_arithmetic.116, f32[4,512,2048]{2,1,0:T(8,128)} %get-tuple-element.240, s32[2048]{0:T(1024)S(1)} %bitcast.148, ...), kind=kOutput, calls=%fused_computation.40.clone.1 | convolution fusion | flops 1115684864 | bytes 37765124 | tf_op jit(solution)/shard_map/while/body/eval_jaxpr/hqk,khd->hqd/dot_general | solution.py:86
  335.4 18.0 %shift_right_arithmetic.116 = s32[4,512,2048]{2,1,0:T(8,128)} reshape(s32[4,512,8,256]{3,2,1,0:T(8,128)} %shift_right_arithmetic.115) | data formatting | bytes 33554432 | tf_op jit(solution)/shard_map/while/body/eval_jaxpr/shift_right_arithmetic | solution.py:19
  355.2 10.9 %fusion.86 = (f32[4,512]{1,0:T(4,128)S(1)}, f32[4,512,2048]{2,1,0:T(8,128)}) fusion(pred[512,2048]{1,0:T(8,128)(4,1)S(1)} %broadcast_compare_fusion.3, bf16[2048,4,128]{2,0,1:T(8,128)(2,1)} %get-tuple-element.276, bf16[4,512,4,128]{3,1,2,0:T(8,128)(2,1)} %get-tuple-element.275, s32[]{:T(128)S(6)} %copy.100), kind=kOutput, calls=%fused_computation.33.clone.1 | convolution fusion | flops 1086322688 | bytes 20455428 | tf_op jit(solution)/shard_map/while/body/eval_jaxpr/qhd,khd->hqk/dot_general | solution.py:75
  366.2 15.4 %fusion.87 = f32[4,4,512,128]{3,2,0,1:T(8,128)} fusion(f32[4,4,512,128]{3,2,0,1:T(8,128)} %get-tuple-element.258, s32[]{:T(128)S(6)} %copy.100, bf16[2048,4,128]{2,0,1:T(8,128)(2,1)S(1)} %copy-done.3, s32[4,512,2048]{2,1,0:T(8,128)} %shift_right_arithmetic.116, f32[4,512,2048]{2,1,0:T(8,128)} %get-tuple-element.240, s32[2048]{0:T(1024)S(1)} %bitcast.148, ...), kind=kOutput, calls=%fused_computation.40.clone.1 | convolution fusion | flops 1115684864 | bytes 37765124 | tf_op jit(solution)/shard_map/while/body/eval_jaxpr/hqk,khd->hqd/dot_general | solution.py:86
  398.9 18.0 %shift_right_arithmetic.116 = s32[4,512,2048]{2,1,0:T(8,128)} reshape(s32[4,512,8,256]{3,2,1,0:T(8,128)} %shift_right_arithmetic.115) | data formatting | bytes 33554432 | tf_op jit(solution)/shard_map/while/body/eval_jaxpr/shift_right_arithmetic | solution.py:19
  418.7 10.9 %fusion.86 = (f32[4,512]{1,0:T(4,128)S(1)}, f32[4,512,2048]{2,1,0:T(8,128)}) fusion(pred[512,2048]{1,0:T(8,128)(4,1)S(1)} %broadcast_compare_fusion.3, bf16[2048,4,128]{2,0,1:T(8,128)(2,1)} %get-tuple-element.276, bf16[4,512,4,128]{3,1,2,0:T(8,128)(2,1)} %get-tuple-element.275, s32[]{:T(128)S(6)} %copy.100), kind=kOutput, calls=%fused_computation.33.clone.1 | convolution fusion | flops 1086322688 | bytes 20455428 | tf_op jit(solution)/shard_map/while/body/eval_jaxpr/qhd,khd->hqk/dot_general | solution.py:75
  429.7 15.4 %fusion.87 = f32[4,4,512,128]{3,2,0,1:T(8,128)} fusion(f32[4,4,512,128]{3,2,0,1:T(8,128)} %get-tuple-element.258, s32[]{:T(128)S(6)} %copy.100, bf16[2048,4,128]{2,0,1:T(8,128)(2,1)S(1)} %copy-done.3, s32[4,512,2048]{2,1,0:T(8,128)} %shift_right_arithmetic.116, f32[4,512,2048]{2,1,0:T(8,128)} %get-tuple-element.240, s32[2048]{0:T(1024)S(1)} %bitcast.148, ...), kind=kOutput, calls=%fused_computation.40.clone.1 | convolution fusion | flops 1115684864 | bytes 37765124 | tf_op jit(solution)/shard_map/while/body/eval_jaxpr/hqk,khd->hqd/dot_general | solution.py:86
  453.5 23.6 %pmax.7 = f32[4,2048]{1,0:T(4,128)S(1)} all-reduce(f32[4,2048]{1,0:T(4,128)S(1)} %bitcast.149), channel_id=1, replica_groups=mesh['seq'=8,'head'=4] {'seq'}, use_global_device_ids=true, to_apply=%region_6.7 | all-reduce | flops 8192 | bytes 65536 | tf_op jit(solution)/shard_map/pmax | solution.py:98
  482.5 66.7 %reduce-scatter.13.cloned.1.call-done = bf16[256,4]{1,0:T(8,128)(2,1)} async-done(((bf16[2048,4]{1,0:T(8,128)(2,1)}), bf16[256,4]{1,0:T(8,128)(2,1)}) %reduce-scatter.13.cloned.1.call-update) | async-done | bytes 2064
  550.1 71.0 %reduce-scatter.7.cloned.1.call-done = bf16[4,256,128]{2,1,0:T(8,128)(2,1)} async-done(((bf16[4,2048,128]{2,1,0:T(8,128)(2,1)}), bf16[4,256,128]{2,1,0:T(8,128)(2,1)}) %reduce-scatter.7.cloned.1.call-update) | async-done | bytes 262160 | tf_op jit(solution)/shard_map/reduce_scatter | solution.py:101
  626.3 23.9 %reduce-scatter.9.cloned.1.call-done = bf16[256,512]{0,1:T(8,128)(2,1)} async-done(((bf16[256,2048]{0,1:T(8,128)(2,1)}), bf16[256,512]{0,1:T(8,128)(2,1)}) %reduce-scatter.9.cloned.1.call-update) | async-done | bytes 262160 | tf_op jit(solution)/shard_map/reduce_scatter | solution.py:123
  658.0 17.9 %all-gather.4.cloned.1.call-done = bf16[256,2048]{0,1:T(8,128)(2,1)} async-done(((bf16[256,512]{0,1:T(8,128)(2,1)}), bf16[256,2048]{0,1:T(8,128)(2,1)}) %all-gather.4.cloned.1.call-update) | async-done | bytes 1048592 | tf_op jit(solution)/shard_map/all_gather | solution.py:132
  693.3 33.1 %all-gather.6.cloned.1.call-done = bf16[2048,512]{1,0:T(8,128)(2,1)} async-done(((bf16[256,512]{1,0:T(8,128)(2,1)}), bf16[2048,512]{1,0:T(8,128)(2,1)}) %all-gather.6.cloned.1.call-update) | async-done | bytes 2097168 | tf_op jit(solution)/shard_map/all_gather | solution.py:151
  726.3 49.8 %all-gather.8.cloned.1.call-done = bf16[2048,512]{1,0:T(8,128)(2,1)} async-done(((bf16[256,512]{1,0:T(8,128)(2,1)}), bf16[2048,512]{1,0:T(8,128)(2,1)}) %all-gather.8.cloned.1.call-update) | async-done | bytes 2097168 | tf_op jit(solution)/shard_map/all_gather | solution.py:152
  776.1 49.9 %conditional.1 = (f32[4,256]{1,0:T(4,128)S(1)}, f32[4,256,128]{1,2,0:T(8,128)}) conditional(s32[]{:T(128)} %convert_element_type.119, () %tuple.18, (s32[2048]{0:T(1024)S(1)}, s32[256]{0:T(256)S(1)}, bf16[256,512]{1,0:T(8,128)(2,1)S(1)}, bf16[2048,512]{1,0:T(8,128)(2,1)}, s32[2048]{0:T(1024)S(1)}, /*index=5*/s32[2048]{0:T(1024)S(1)}, ...), branch_computations={%region_13.14_spmd, %region_14.17_spmd} | conditional | flops 1107840000 | bytes 107811880 | solution.py:182
  783.2 22.2 %gather_fusion = f32[2048,4,256]{2,1,0:T(4,128)} fusion(f32[4,256,2048]{1,0,2:T(4,128)} %get-tuple-element.76, s32[2048]{0:T(1024)S(1)} %fusion.17), kind=kCustom, calls=%fused_computation | custom fusion | bytes 16785408 | tf_op jit(solution)/shard_map/cond/branch_1_fun/jit(_take)/gather | solution.py:171
  830.8 25.3 %reduce-scatter.11.cloned.1.call-done = bf16[256,512]{0,1:T(8,128)(2,1)} async-done(((bf16[256,2048]{0,1:T(8,128)(2,1)}), bf16[256,512]{0,1:T(8,128)(2,1)}) %reduce-scatter.11.cloned.1.call-update) | async-done | bytes 262160 | tf_op jit(solution)/shard_map/reduce_scatter | solution.py:190
  (134 shorter events, 206.0 us)
Async XLA Ops:
  6.5 12.2 %copy-start = (bf16[2048,512]{1,0:T(8,128)(2,1)S(1)}, bf16[2048,512]{1,0:T(8,128)(2,1)}, u32[]{:S(2)}) copy-start(bf16[2048,512]{1,0:T(8,128)(2,1)} %param.17) | copy-start | bytes 6291460
  6.5 181.6 %all-reduce.2.cloned.1.call-start = ((), (), s32[]{:S(2)}) async-start(), calls=%async_computation.4 | async-start | bytes 8388608 | tf_op jit(solution)/shard_map/psum | solution.py:14
  32.6 516.6 %reduce-scatter.13.cloned.1.call-start = ((), (), s32[]{:S(2)}) async-start(), calls=%async_computation.11 | async-start | bytes 589824
  228.2 11.0 %copy-start.3 = (bf16[2048,4,128]{2,0,1:T(8,128)(2,1)S(1)}, bf16[2048,4,128]{2,0,1:T(8,128)(2,1)}, u32[]{:S(2)}) copy-start(bf16[2048,4,128]{2,0,1:T(8,128)(2,1)} %get-tuple-element.278) | copy-start | bytes 6291460 | tf_op jit(solution)/shard_map/while
  291.7 11.0 %copy-start.3 = (bf16[2048,4,128]{2,0,1:T(8,128)(2,1)S(1)}, bf16[2048,4,128]{2,0,1:T(8,128)(2,1)}, u32[]{:S(2)}) copy-start(bf16[2048,4,128]{2,0,1:T(8,128)(2,1)} %get-tuple-element.278) | copy-start | bytes 6291460 | tf_op jit(solution)/shard_map/while
  355.2 11.0 %copy-start.3 = (bf16[2048,4,128]{2,0,1:T(8,128)(2,1)S(1)}, bf16[2048,4,128]{2,0,1:T(8,128)(2,1)}, u32[]{:S(2)}) copy-start(bf16[2048,4,128]{2,0,1:T(8,128)(2,1)} %get-tuple-element.278) | copy-start | bytes 6291460 | tf_op jit(solution)/shard_map/while
  418.7 11.0 %copy-start.3 = (bf16[2048,4,128]{2,0,1:T(8,128)(2,1)S(1)}, bf16[2048,4,128]{2,0,1:T(8,128)(2,1)}, u32[]{:S(2)}) copy-start(bf16[2048,4,128]{2,0,1:T(8,128)(2,1)} %get-tuple-element.278) | copy-start | bytes 6291460 | tf_op jit(solution)/shard_map/while
  478.2 142.9 %reduce-scatter.7.cloned.1.call-start = ((), (), s32[]{:S(2)}) async-start(), calls=%async_computation.5 | async-start | bytes 2359296 | tf_op jit(solution)/shard_map/reduce_scatter | solution.py:101
  478.3 144.2 %copy-start.4 = (bf16[512,2048]{1,0:T(8,128)(2,1)S(1)}, bf16[512,2048]{1,0:T(8,128)(2,1)}, u32[]{:S(2)}) copy-start(bf16[512,2048]{1,0:T(8,128)(2,1)} %param.20) | copy-start | bytes 6291460
  482.4 167.7 %reduce-scatter.9.cloned.1.call-start = ((), (), s32[]{:S(2)}) async-start(), calls=%async_computation.6 | async-start | bytes 1310720 | tf_op jit(solution)/shard_map/reduce_scatter | solution.py:123
  624.4 51.6 %all-gather.4.cloned.1.call-start = ((), (), s32[]{:S(2)}) async-start(), calls=%async_computation.7 | async-start | bytes 1310720 | tf_op jit(solution)/shard_map/all_gather | solution.py:132
  658.0 68.3 %all-gather.6.cloned.1.call-start = ((), (), s32[]{:S(2)}) async-start(), calls=%async_computation.8 | async-start | bytes 2359296 | tf_op jit(solution)/shard_map/all_gather | solution.py:151
  675.9 3.5 copy-start.6
  679.4 96.7 %all-gather.8.cloned.1.call-start = ((), (), s32[]{:S(2)}) async-start(), calls=%async_computation.9 | async-start | bytes 2359296 | tf_op jit(solution)/shard_map/all_gather | solution.py:152
  682.5 173.5 %reduce-scatter.11.cloned.1.call-start = ((), (), s32[]{:S(2)}) async-start(), calls=%async_computation.10 | async-start | bytes 1310720 | tf_op jit(solution)/shard_map/reduce_scatter | solution.py:190
  685.3 7.2 copy-start.5
  685.3 7.2 copy-start.7
  779.9 3.2 copy-start.2
  826.0 33.6 %copy-start.1 = (bf16[2048,512]{1,0:T(8,128)(2,1)S(1)}, bf16[2048,512]{1,0:T(8,128)(2,1)}, u32[]{:S(2)}) copy-start(bf16[2048,512]{1,0:T(8,128)(2,1)} %param.17) | copy-start | bytes 6291460
Sparse Core Ops, SparseCore 0:
  32.7 155.3 all-reduce.1
  478.3 70.7 reduce-scatter.12
  552.7 68.3 reduce-scatter.6
  624.5 25.6 reduce-scatter.8
  658.1 17.7 all-gather.3
  679.5 46.7 all-gather.5
  728.4 47.6 all-gather.7
  830.9 25.0 reduce-scatter.10
where the time goes:
time: 877 us; the launch traced here: 867 us
  waiting for transfers between devices  420 us (48%)
  local copies, waits for them, and re-layouts  173 us (20%)
  matrix products  160 us (18%)
  other arithmetic  66.6 us (8%)
  blocking collectives  29.5 us (3%)
  between operations  14.6 us (2%)
    psum x1, waiting for transfers between devices, from_root(): return lax.psum(kept, axis)  132 us
    shift_right_arithmetic x14, local copies, waits for them, and re-layouts, unpack_bits(): jnp.right_shift(packed_words[..., None, :], shifts[:, None])  108 us
    reduce_scatter x1, waiting for transfers between devices, per_device(): lax.psum_scatter((summed * factor[..., None]).astype(jnp.bfloat16), 'seq'...  71 us
    unnamed x9, waiting for transfers between devices  66.8 us
    dot_general x4, matrix products, cross_block(): jnp.einsum('hqk,khd->hqd', weights, value_heads, preferred_element_type=j...  61.8 us
    all_gather x1, waiting for transfers between devices, per_device(): value_piece = lax.all_gather(latent_values, 'seq', axis=0, tiled=True)  49.8 us
    dot_general x4, matrix products, cross_block(): jnp.einsum('qhd,khd->hqk', query_block, key_heads, preferred_element_type...  43.7 us
    reduce_sum x4, other arithmetic, cross_block(): row_sum = jnp.sum(exponent, axis=-1)  33.5 us
  transfers between devices with their start and end apart: 8, of which 8 were waited for; matrix products, arithmetic and copies ran while one was open for 5% of the time, Pallas kernels for 0%

commit v1 on v0

v1 whole, which is shorter than its diff:
```python
import functools
import math

import jax
import jax.numpy as jnp
from jax import lax
from jax.experimental import pallas as pl
from jax.experimental.pallas import tpu as pltpu
from jax.sharding import PartitionSpec as P

keep_scale = 8.0 / 7.0
masked = -1e30
log2e = 1.4426950408889634
MESH = pl.DeviceIdType.MESH
ANY = pl.BlockSpec(memory_space=pl.ANY)


def unpack_bits(packed_words, word_bits):
    shifts = jnp.arange(word_bits, dtype=jnp.int32)
    bit_table = jnp.bitwise_and(jnp.right_shift(packed_words[..., None, :], shifts[:, None]), 1)
    return bit_table.reshape(packed_words.shape[:-1] + (word_bits * packed_words.shape[-1],))


def rms_rows(matrix):
    wide_rows = matrix.astype(jnp.float32)
    mean_square = jnp.mean(wide_rows * wide_rows, axis=-1, keepdims=True)
    return (wide_rows * lax.rsqrt(mean_square + 1e-06)).astype(jnp.bfloat16)


def greet(axis, n, me):
    barrier = pltpu.get_barrier_semaphore()
    for d in range(1, n):
        pl.semaphore_signal(
            barrier, inc=1, device_id={axis: lax.rem(me + d, n)}, device_id_type=MESH
        )
    pl.semaphore_wait(barrier, n - 1)


def exchange_kernel(axis, n, modes, widths, *refs):
    count = len(modes)
    ins, outs = refs[:count], refs[count : 2 * count]
    send_sem, recv_sem, local_sem = refs[2 * count :]
    me = lax.axis_index(axis)

    def piece(a, j):
        if modes[a] == "lead":
            return ins[a].at[j]
        if modes[a] == "cols":
            start = pl.multiple_of(j * widths[a], 128)
            return ins[a].at[:, pl.ds(start, widths[a])]
        return ins[a]

    local = []
    for a in range(count):
        copy = pltpu.make_async_copy(piece(a, me), outs[a].at[me], local_sem.at[a])
        copy.start()
        local.append(copy)
    greet(axis, n, me)
    copies = []
    for d in range(1, n):
        to = lax.rem(me + d, n)
        for a in range(count):
            copy = pltpu.make_async_remote_copy(
                src_ref=piece(a, to),
                dst_ref=outs[a].at[me],
                send_sem=send_sem.at[a, d],
                recv_sem=recv_sem.at[a, d],
                device_id={axis: to},
                device_id_type=MESH,
            )
            copy.start()
            copies.append(copy)
    for copy in copies:
        copy.wait()
    for copy in local:
        copy.wait()


def exchange(arrays, modes, axis, ident):
    n = lax.axis_size(axis)
    shapes, widths = [], []
    for x, mode in zip(arrays, modes):
        if mode == "lead":
            shape, width = x.shape, 0
        elif mode == "cols":
            width = x.shape[1] // n
            shape = (n, x.shape[0], width)
        else:
            shape, width = (n,) + x.shape, 0
        shapes.append(jax.ShapeDtypeStruct(shape, x.dtype))
        widths.append(width)
    return pl.pallas_call(
        functools.partial(exchange_kernel, axis, n, tuple(modes), tuple(widths)),
        out_shape=tuple(shapes),
        in_specs=[ANY] * len(arrays),
        out_specs=tuple([ANY] * len(arrays)),
        scratch_shapes=[
            pltpu.SemaphoreType.DMA((len(arrays), n)),
            pltpu.SemaphoreType.DMA((len(arrays), n)),
            pltpu.SemaphoreType.DMA((len(arrays),)),
        ],
        compiler_params=pltpu.CompilerParams(collective_id=ident, has_side_effects=True),
    )(*arrays)


def spread_kernel(axis, n, x_ref, out_ref, send_a, recv_a, send_b, recv_b, local_sem):
    me = lax.axis_index(axis)
    root = n - 1
    greet(axis, n, me)

    def parts(j):
        return (pl.ds(j * n, n), pl.ds(root * n + j, 1))

    tail = pl.ds(root * n + root, 1)

    def remote(src, dst, send, recv, to):
        return pltpu.make_async_remote_copy(
            src_ref=src,
            dst_ref=dst,
            send_sem=send,
            recv_sem=recv,
            device_id={axis: to},
            device_id_type=MESH,
        )

    @pl.when(me == root)
    def _():
        copies = []
        for j in range(root):
            for p, part in enumerate(parts(j)):
                copies.append(
                    remote(x_ref.at[part], out_ref.at[part], send_a.at[p, j], recv_a.at[p], j)
                )
                copies[-1].start()
        for j in range(root):
            copies.append(
                remote(x_ref.at[tail], out_ref.at[tail], send_a.at[2, j], recv_a.at[2], j)
            )
            copies[-1].start()
        own = pltpu.make_async_copy(x_ref, out_ref, local_sem)
        own.start()
        for copy in copies:
            copy.wait_send()
        own.wait()

    @pl.when(me != root)
    def _():
        copies = []
        for p, part in enumerate(parts(me)):
            remote(x_ref.at[part], out_ref.at[part], send_a.at[p, 0], recv_a.at[p], root).wait_recv()
            for d in range(1, root):
                to = lax.rem(me + d, root)
                copies.append(
                    remote(
                        out_ref.at[part], out_ref.at[part], send_b.at[p, d], recv_b.at[p, d], to
                    )
                )
                copies[-1].start()
        remote(x_ref.at[tail], out_ref.at[tail], send_a.at[2, 0], recv_a.at[2], root).wait_recv()
        for copy in copies:
            copy.wait()


def spread(x, axis, ident):
    n = lax.axis_size(axis)
    rows, width = x.shape
    grains = x.reshape(n * n, rows // (n * n), width)
    out = pl.pallas_call(
        functools.partial(spread_kernel, axis, n),
        out_shape=jax.ShapeDtypeStruct(grains.shape, x.dtype),
        in_specs=[ANY],
        out_specs=ANY,
        scratch_shapes=[
            pltpu.SemaphoreType.DMA((3, n)),
            pltpu.SemaphoreType.DMA((3,)),
            pltpu.SemaphoreType.DMA((2, n)),
            pltpu.SemaphoreType.DMA((2, n)),
            pltpu.SemaphoreType.DMA,
        ],
        compiler_params=pltpu.CompilerParams(collective_id=ident, has_side_effects=True),
    )(grains)
    return out.reshape(rows, width)


def dot_t(a, b):
    return lax.dot_general(a, b, (((1,), (1,)), ((), ())), preferred_element_type=jnp.float32)


def fold_lanes(x, op):
    parts = [x[:, j : j + 128] for j in range(0, x.shape[1], 128)]
    return functools.reduce(op, parts)


def cross_kernel(n, hd, scale, q_ref, k_ref, v_ref, w_ref, o_ref, st_ref, s_ref):
    block, head = pl.program_id(0), pl.program_id(1)
    bq = q_ref.shape[0]
    keys = k_ref.shape[0]
    chunk = w_ref.shape[2]
    chunks = keys // chunk
    root = lax.axis_index("seq") == n - 1
    cols = pl.ds(pl.multiple_of(head * hd, 128), hd)
    factor = scale * log2e

    def finish(acc, top, total):
        o_ref[...] = (acc * (keep_scale / total)).astype(o_ref.dtype)
        stat = top * scale + jnp.log(total)
        lane = lax.broadcasted_iota(jnp.int32, st_ref.shape, 1)
        st_ref[...] = jnp.where(lane == head, stat, st_ref[...])

    @pl.when(head == 0)
    def _():
        st_ref[...] = jnp.zeros_like(st_ref)

    @pl.when(jnp.logical_not(root))
    def _():
        q = q_ref[...]
        tops = None
        for c in range(chunks):
            s = dot_t(q, k_ref[c * chunk : (c + 1) * chunk, cols])
            s_ref[c] = s
            t = fold_lanes(s, jnp.maximum)
            tops = t if tops is None else jnp.maximum(tops, t)
        top = jnp.max(tops, axis=1, keepdims=True)
        words = w_ref[0]
        acc = jnp.zeros((bq, hd), jnp.float32)
        sums = jnp.zeros((bq, 128), jnp.float32)
        for c in range(chunks):
            e = jnp.exp2((s_ref[c] - top) * factor)
            sums = sums + fold_lanes(e, jnp.add)
            weights = jnp.where((words & (1 << c)) != 0, e, 0.0).astype(jnp.bfloat16)
            acc = acc + jnp.dot(
                weights,
                v_ref[c * chunk : (c + 1) * chunk, cols],
                preferred_element_type=jnp.float32,
            )
        finish(acc, top, jnp.sum(sums, axis=1, keepdims=True))

    @pl.when(root)
    def _():
        q = q_ref[...]
        used = jnp.minimum(((block + 1) * bq + chunk - 1) // chunk, chunks)
        row = block * bq + lax.broadcasted_iota(jnp.int32, (bq, chunk), 0)
        lane = lax.broadcasted_iota(jnp.int32, (bq, chunk), 1)

        def first(c, tops):
            at = pl.ds(pl.multiple_of(c * chunk, chunk), chunk)
            s = dot_t(q, k_ref[at, cols])
            s = jnp.where(lane + c * chunk <= row, s, masked)
            s_ref[c] = s
            return jnp.maximum(tops, fold_lanes(s, jnp.maximum))

        tops = lax.fori_loop(0, used, first, jnp.full((bq, 128), masked, jnp.float32))
        top = jnp.max(tops, axis=1, keepdims=True)
        words = w_ref[0]

        def second(c, carry):
            acc, sums = carry
            at = pl.ds(pl.multiple_of(c * chunk, chunk), chunk)
            e = jnp.exp2((s_ref[c] - top) * factor)
            e = jnp.where(lane + c * chunk <= row, e, 0.0)
            sums = sums + fold_lanes(e, jnp.add)
            weights = jnp.where((words & (1 << c)) != 0, e, 0.0).astype(jnp.bfloat16)
            acc = acc + jnp.dot(weights, v_ref[at, cols], preferred_element_type=jnp.float32)
            return acc, sums

        acc, sums = lax.fori_loop(
            0,
            used,
            second,
            (jnp.zeros((bq, hd), jnp.float32), jnp.zeros((bq, 128), jnp.float32)),
        )
        finish(acc, top, jnp.sum(sums, axis=1, keepdims=True))


def cross_attention(queries, keys, values, words, n, hd):
    rows, width = queries.shape
    toks = keys.shape[0]
    heads = width // hd
    bq = min(256, rows)
    chunk = words.shape[2]
    return pl.pallas_call(
        functools.partial(cross_kernel, n, hd, 1.0 / math.sqrt(hd)),
        grid=(rows // bq, heads),
        in_specs=[
            pl.BlockSpec((bq, hd), lambda i, h: (i, h)),
            pl.BlockSpec((toks, width), lambda i, h: (0, 0)),
            pl.BlockSpec((toks, width), lambda i, h: (0, 0)),
            pl.BlockSpec((1, bq, chunk), lambda i, h: (h, i, 0)),
        ],
        out_specs=(
            pl.BlockSpec((bq, hd), lambda i, h: (i, h)),
            pl.BlockSpec((bq, 128), lambda i, h: (i, 0)),
        ),
        out_shape=(
            jax.ShapeDtypeStruct((rows, width), jnp.bfloat16),
            jax.ShapeDtypeStruct((rows, 128), jnp.float32),
        ),
        scratch_shapes=[pltpu.VMEM((toks // chunk, bq, chunk), jnp.float32)],
        cost_estimate=pl.CostEstimate(
            flops=4 * rows * toks * width * 4,
            transcendentals=heads * rows * toks,
            bytes_accessed=4 * heads * rows * chunk,
        ),
    )(queries, keys, values, words)


def latent_kernel(hd, scale, q_ref, k_ref, v_ref, w_ref, o_ref, s_ref):
    rows = q_ref.shape[0]
    pieces, piece_rows = k_ref.shape[0], k_ref.shape[1]
    chunk = w_ref.shape[2]
    factor = scale * log2e
    first_row = lax.axis_index("seq") * rows
    used = first_row + rows
    row = first_row + lax.broadcasted_iota(jnp.int32, (rows, chunk), 0)
    lane = lax.broadcasted_iota(jnp.int32, (rows, chunk), 1)
    per = piece_rows // chunk
    q = q_ref[...]
    words = w_ref[0]
    tops = jnp.full((rows, 128), masked, jnp.float32)
    for p in range(pieces):
        s = dot_t(q, k_ref[p])
        for j in range(per):
            c = p * per + j
            part = jnp.where(lane + c * chunk <= row, s[:, j * chunk : (j + 1) * chunk], masked)
            s_ref[c] = part
            tops = jnp.maximum(tops, part)
    top = jnp.max(tops, axis=1, keepdims=True)
    acc = jnp.zeros((rows, hd), jnp.float32)
    sums = jnp.zeros((rows, 128), jnp.float32)
    for p in range(pieces):
        kept = []
        for j in range(per):
            c = p * per + j
            e = jnp.exp2((s_ref[c] - top) * factor)
            e = jnp.where(lane + c * chunk <= row, e, 0.0)
            sums = sums + e
            kept.append(jnp.where((words & (1 << c)) != 0, e, 0.0).astype(jnp.bfloat16))
        weights = jnp.concatenate(kept, axis=1) if per > 1 else kept[0]
        acc = acc + jnp.dot(weights, v_ref[p], preferred_element_type=jnp.float32)
    total = jnp.sum(sums, axis=1, keepdims=True)
    o_ref[...] = (acc * (keep_scale / total)).astype(o_ref.dtype)


def latent_attention(queries, keys, values, words, hd):
    rows, width = queries.shape
    pieces, piece_rows, _ = keys.shape
    heads = width // hd
    chunk = words.shape[2]
    return pl.pallas_call(
        functools.partial(latent_kernel, hd, 1.0 / math.sqrt(hd)),
        grid=(heads,),
        in_specs=[
            pl.BlockSpec((rows, hd), lambda h: (0, h)),
            pl.BlockSpec((pieces, piece_rows, hd), lambda h: (0, 0, h)),
            pl.BlockSpec((pieces, piece_rows, hd), lambda h: (0, 0, h)),
            pl.BlockSpec((1, rows, chunk), lambda h: (h, 0, 0)),
        ],
        out_specs=pl.BlockSpec((rows, hd), lambda h: (0, h)),
        out_shape=jax.ShapeDtypeStruct((rows, width), jnp.bfloat16),
        scratch_shapes=[pltpu.VMEM((pieces * piece_rows // chunk, rows, chunk), jnp.float32)],
    )(queries, keys, values, words)


def per_device(
    context,
    wq_cross,
    wk_cross,
    wv_cross,
    wo_cross,
    wq_latent,
    wk_latent,
    wv_latent,
    wo_latent,
    cross_keep,
    latent_keep,
    residual_keep,
):
    seq_count = lax.axis_size("seq")
    seq_index = lax.axis_index("seq")
    head_index = lax.axis_index("head")
    model_width = context.shape[1]
    head_local = cross_keep.shape[0]
    latent_count = cross_keep.shape[1]
    head_dim = wq_cross.shape[1] // head_local
    columns = model_width // lax.axis_size("head")
    local_rows = latent_count // seq_count
    first_row = seq_index * local_rows

    def project(rows, weight):
        return jnp.dot(rows, weight, preferred_element_type=jnp.float32).astype(jnp.bfloat16)

    normed = rms_rows(context)
    own_queries = project(normed[context.shape[0] - latent_count :], wq_cross)
    own_columns = lax.dynamic_slice_in_dim(
        context[context.shape[0] - latent_count :], head_index * columns, columns, 1
    )
    own_columns = jnp.where(seq_index == seq_count - 1, own_columns, 0).astype(jnp.bfloat16)
    inputs = lax.psum_scatter(own_columns, "seq", scatter_dimension=0, tiled=True)
    key_rows = project(normed, wk_cross)
    value_rows = project(normed, wv_cross)
    queries = spread(own_queries, "seq", 1)
    partial, stats = cross_attention(
        queries, key_rows, value_rows, cross_keep, seq_count, head_dim
    )
    packed_stats = stats[:, :8].reshape(seq_count, local_rows, 8).transpose(0, 2, 1)
    partials, levels = exchange(
        [partial.reshape(seq_count, local_rows, head_local * head_dim), packed_stats],
        ["lead", "lead"],
        "seq",
        2,
    )
    levels = levels[:, :head_local, :]
    level_top = jnp.max(levels, axis=0, keepdims=True)
    share = jnp.exp(levels - level_top)
    share = share / jnp.sum(share, axis=0, keepdims=True)
    share = share.transpose(0, 2, 1)[..., None]
    spread_heads = partials.reshape(seq_count, local_rows, head_local, head_dim)
    attended = (
        jnp.sum(spread_heads.astype(jnp.float32) * share, axis=0)
        .reshape(local_rows, head_local * head_dim)
        .astype(jnp.bfloat16)
    )
    residual_rows = lax.dynamic_slice_in_dim(residual_keep, first_row, local_rows, 1)
    residual_mask = lax.dynamic_slice_in_dim(
        unpack_bits(residual_rows, 16), head_index * columns, columns, 2
    ).astype(jnp.float32)
    branches = exchange([project(attended, wo_cross)], ["cols"], "head", 3)[0]
    branch = jnp.sum(branches.astype(jnp.float32), axis=0)
    latents = (
        inputs.astype(jnp.float32) + residual_mask[0] * keep_scale * branch
    ).astype(jnp.bfloat16)
    gathered = exchange([latents], ["all"], "head", 4)[0]
    whole_latents = gathered.transpose(1, 0, 2).reshape(local_rows, model_width)
    normed_latents = rms_rows(whole_latents)
    latent_queries = project(normed_latents, wq_latent)
    latent_keys = project(normed_latents, wk_latent)
    latent_values = project(normed_latents, wv_latent)
    latent_words = lax.dynamic_slice_in_dim(latent_keep, first_row, local_rows, 1)
    all_keys, all_values = exchange([latent_keys, latent_values], ["all", "all"], "seq", 5)
    latent_attended = latent_attention(
        latent_queries, all_keys, all_values, latent_words, head_dim
    )
    latent_branches = exchange([project(latent_attended, wo_latent)], ["cols"], "head", 6)[0]
    latent_branch = jnp.sum(latent_branches.astype(jnp.float32), axis=0)
    return (latents.astype(jnp.float32) + residual_mask[1] * keep_scale * latent_branch).astype(
        jnp.bfloat16
    )


def solution(mesh):
    in_specs = (
        P("seq", None),
        P(None, "head"),
        P(None, "head"),
        P(None, "head"),
        P("head", None),
        P(None, "head"),
        P(None, "head"),
        P(None, "head"),
        P("head", None),
        P("head", None, "seq"),
        P("head", None, None),
        P(),
    )
    out_specs = P("seq", "head")
    return jax.shard_map(
        per_device, mesh=mesh, in_specs=in_specs, out_specs=out_specs, check_vma=False
    )
```

time: 877 us -> 440 us (0.50); the launches traced: 867 us -> 439 us
  waiting for transfers between devices: 420 us -> 0.04 us
  Pallas kernels: 0 us -> 339 us
  local copies, waits for them, and re-layouts: 173 us -> 26 us
  matrix products: 160 us -> 37.3 us
  other arithmetic: 66.6 us -> 23.2 us
  blocking collectives: 29.5 us -> 0 us
    pallas_call x0 -> x8, Pallas kernels: none -> 339 us  [the longest x5 192 us: exchange(): pl.pallas_call(functools.partial(exchange_kernel, axis, n, tuple(modes),...]
    psum x1 -> x0, waiting for transfers between devices: 132 us -> none  [from_root(): return lax.psum(kept, axis)]
    reduce_scatter x3 -> x1, waiting for transfers between devices: 120 us -> 0.02 us  [per_device(): lax.psum_scatter(own_columns, 'seq', scatter_dimension=0, tiled=True)]
    dot_general x17 -> x8, matrix products: 149 us -> 37.3 us  [project(): jnp.dot(rows, weight, preferred_element_type=jnp.float32)]
    all_gather x3 -> x0, waiting for transfers between devices: 101 us -> none  [the longest x1 49.8 us: per_device(): value_piece = lax.all_gather(latent_values, 'seq', axis=0, tiled=True)]
    shift_right_arithmetic x14 -> x3, local copies, waits for them, and re-layouts: 108 us -> 7.21 us  [unpack_bits(): jnp.right_shift(packed_words[..., None, :], shifts[:, None])]
    unnamed x9 -> x1, waiting for transfers between devices: 66.8 us -> 0.02 us
    gather x2 -> x0, local copies, waits for them, and re-layouts: 32.1 us -> none  [update(): keep_flags = jnp.take(latent_mask, key_index, axis=2)]
  transfers between devices with their start and end apart: 8 -> 1, of which waited for: 8 -> 0; matrix products, arithmetic and copies ran while one was open for 5% -> 15% of each run, Pallas kernels for 0% -> 47%
where the time goes in v1:
time: 440 us; the launch traced here: 439 us
  Pallas kernels  339 us (77%)
  matrix products  37.3 us (8%)
  local copies, waits for them, and re-layouts  26 us (6%)
  other arithmetic  23.2 us (5%)
  between operations  13.6 us (3%)
    pallas_call x5, Pallas kernels, exchange(): pl.pallas_call(functools.partial(exchange_kernel, axis, n, tuple(modes),...  192 us
    pallas_call x1, Pallas kernels, spread(): pl.pallas_call(functools.partial(spread_kernel, axis, n), out_shape=jax.S...  96.9 us
    pallas_call x1, Pallas kernels, cross_attention(): pl.pallas_call(functools.partial(cross_kernel, n, hd, 1.0 / math.sqrt(hd)...  42.1 us
    dot_general x8, matrix products, project(): jnp.dot(rows, weight, preferred_element_type=jnp.float32)  37.3 us
    mul x2, local copies, waits for them, and re-layouts, per_device(): spread_heads.astype(jnp.float32) * share  9.44 us
  transfers between devices with their start and end apart: 1, of which 0 were waited for; matrix products, arithmetic and copies ran while one was open for 15% of the time, Pallas kernels for 47%

profile of v1, /device:TPU:11, one launch (start us, length us, event | category | flops | bytes accessed | tf_op | source)
XLA Modules:
  0.0 439.1 jit_solution(17774854413603463754)
XLA Ops:
  6.5 3.5 dynamic-slice_select_fusion
  10.1 5.1 %fusion = f32[2048]{0:T(1024)S(1)} fusion(bf16[2048,2048]{1,0:T(8,128)(2,1)} %param.12), kind=kLoop, calls=%fused_computation.2 | loop fusion | flops 12580864 | bytes 8396800 | tf_op jit(solution)/shard_map/reduce_sum | solution.py:26
  15.2 9.5 %convolution_convert_fusion.2 = bf16[2048,512]{1,0:T(8,128)(2,1)} fusion(bf16[2048,512]{1,0:T(8,128)(2,1)S(1)} %copy-done, bf16[2048,2048]{1,0:T(8,128)(2,1)} %param.12, f32[2048]{0:T(1024)S(1)} %add_rsqrt_fusion), kind=kOutput, calls=%fused_computation.7 | convolution fusion | flops 4308598784 | bytes 12591104 | tf_op jit(solution)/shard_map/dot_general | solution.py:390
  24.6 96.9 %shard_map.118 = bf16[64,32,512]{2,1,0:T(8,128)(2,1)} custom-call(bf16[64,32,512]{2,1,0:T(8,128)(2,1)} %bitcast.50), custom_call_target="tpu_custom_call" | custom-call | tf_op jit(solution)/shard_map/pallas_call | solution.py:168
  121.6 9.7 %convolution_convert_fusion.v_ref = bf16[2048,512]{1,0:T(8,128)(2,1)} fusion(bf16[2048,512]{1,0:T(8,128)(2,1)S(1)} %copy-done.8, bf16[2048,2048]{1,0:T(8,128)(2,1)} %param.12, f32[2048]{0:T(1024)S(1)} %add_rsqrt_fusion), kind=kOutput, calls=%fused_computation.5 | convolution fusion | flops 4308598784 | bytes 12591104 | tf_op jit(solution)/shard_map/dot_general | solution.py:390
  131.3 9.5 %convolution_convert_fusion.1.k_ref = bf16[2048,512]{1,0:T(8,128)(2,1)} fusion(bf16[2048,512]{1,0:T(8,128)(2,1)S(1)} %copy-done.9, bf16[2048,2048]{1,0:T(8,128)(2,1)} %param.12, f32[2048]{0:T(1024)S(1)} %add_rsqrt_fusion), kind=kOutput, calls=%fused_computation.6 | convolution fusion | flops 4308598784 | bytes 12591104 | tf_op jit(solution)/shard_map/dot_general | solution.py:390
  140.8 42.1 %shard_map.119 = (bf16[2048,512]{1,0:T(8,128)(2,1)}, f32[2048,128]{1,0:T(8,128)}) custom-call(bf16[2048,512]{1,0:T(8,128)(2,1)} %bitcast.49, bf16[2048,512]{1,0:T(8,128)(2,1)} %convolution_convert_fusion.1.k_ref, bf16[2048,512]{1,0:T(8,128)(2,1)} %convolution_convert_fusion.v_ref, s32[4,2048,256]{2,1,0:T(8,128)} %w_ref.1), custom_call_target="tpu_custom_call" | custom-call | flops 34359738368 | bytes 8388608 | tf_op jit(solution)/shard_map/pallas_call | solution.py:281
  182.9 2.2 copy.14
  185.1 53.9 %shard_map.120 = (bf16[8,256,512]{2,1,0:T(8,128)(2,1)}, f32[8,8,256]{2,1,0:T(8,128)}) custom-call(bf16[8,256,512]{2,1,0:T(8,128)(2,1)} %bitcast.48, f32[8,8,256]{2,1,0:T(8,128)} %bitcast.52), custom_call_target="tpu_custom_call" | custom-call | tf_op jit(solution)/shard_map/pallas_call | solution.py:92
  241.9 3.8 mul.67
  245.7 5.6 %mul.68 = f32[8,256,512]{2,1,0:T(8,128)} reshape(f32[8,256,4,128]{3,2,1,0:T(4,128)} %mul.67) | data formatting | bytes 8388608 | tf_op jit(solution)/shard_map/mul | solution.py:419
  251.4 3.0 multiply_reduce_fusion
  256.1 14.4 %shard_map.121 = bf16[4,256,512]{2,1,0:T(8,128)(2,1)} custom-call(bf16[256,2048]{1,0:T(8,128)(2,1)} %convolution_convert_fusion.4.refs_0_), custom_call_target="tpu_custom_call" | custom-call | tf_op jit(solution)/shard_map/pallas_call | solution.py:92
  271.5 2.2 shift_right_arithmetic.20
  273.8 5.0 %shift_right_arithmetic.21 = s32[2,256,2048]{2,1,0:T(8,128)} reshape(s32[2,256,16,128]{3,2,1,0:T(8,128)} %shift_right_arithmetic.20) | data formatting | bytes 8388608 | tf_op jit(solution)/shard_map/shift_right_arithmetic | solution.py:20
  278.8 1.9 constant_dynamic-slice_fusion.w_ref
  282.2 1.8 fusion.13.refs_0_
  284.0 14.0 %shard_map.122 = bf16[4,256,512]{2,1,0:T(8,128)(2,1)} custom-call(bf16[256,512]{1,0:T(8,128)(2,1)} %fusion.13.refs_0_), custom_call_target="tpu_custom_call" | custom-call | tf_op jit(solution)/shard_map/pallas_call | solution.py:92
  298.1 3.0 convert_bitcast_fusion
  301.3 2.1 copy.16
  309.7 95.1 %shard_map.123 = (bf16[8,256,512]{2,1,0:T(8,128)(2,1)}, bf16[8,256,512]{2,1,0:T(8,128)(2,1)}) custom-call(bf16[256,512]{1,0:T(8,128)(2,1)} %convolution_convert_fusion.6.refs_0_, bf16[256,512]{1,0:T(8,128)(2,1)} %convolution_convert_fusion.5.refs_1_), custom_call_target="tpu_custom_call" | custom-call | tf_op jit(solution)/shard_map/pallas_call | solution.py:92
  404.8 8.2 %shard_map.124 = bf16[256,512]{1,0:T(8,128)(2,1)} custom-call(bf16[256,512]{1,0:T(8,128)(2,1)} %convolution_convert_fusion.7.q_ref, bf16[8,256,512]{2,1,0:T(8,128)(2,1)} %get-tuple-element.15.k_ref, bf16[8,256,512]{2,1,0:T(8,128)(2,1)} %get-tuple-element.16.v_ref, s32[4,256,128]{2,1,0:T(8,128)} %constant_dynamic-slice_fusion.w_ref), custom_call_target="tpu_custom_call" | custom-call | tf_op jit(solution)/shard_map/pallas_call | solution.py:349
  413.0 2.7 convolution_convert_fusion.3.refs_0_
  415.6 14.3 %shard_map.125 = bf16[4,256,512]{2,1,0:T(8,128)(2,1)} custom-call(bf16[256,2048]{1,0:T(8,128)(2,1)} %convolution_convert_fusion.3.refs_0_), custom_call_target="tpu_custom_call" | custom-call | tf_op jit(solution)/shard_map/pallas_call | solution.py:92
  (48 shorter events, 16.1 us)
Async XLA Ops:
  6.5 8.6 %copy-start = (bf16[2048,512]{1,0:T(8,128)(2,1)S(1)}, bf16[2048,512]{1,0:T(8,128)(2,1)}, u32[]{:S(2)}) copy-start(bf16[2048,512]{1,0:T(8,128)(2,1)} %param.13) | copy-start | bytes 6291460
  6.5 275.7 %reduce-scatter.2.cloned.1.call-start = ((), (), s32[]{:S(2)}) async-start(), calls=%async_computation.1 | async-start | bytes 2359296 | tf_op jit(solution)/shard_map/reduce_scatter | solution.py:398
  24.6 96.9 %copy-start.8 = (bf16[2048,512]{1,0:T(8,128)(2,1)S(1)}, bf16[2048,512]{1,0:T(8,128)(2,1)}, u32[]{:S(2)}) copy-start(bf16[2048,512]{1,0:T(8,128)(2,1)} %param.15) | copy-start | bytes 6291460
  121.6 9.7 %copy-start.9 = (bf16[2048,512]{1,0:T(8,128)(2,1)S(1)}, bf16[2048,512]{1,0:T(8,128)(2,1)}, u32[]{:S(2)}) copy-start(bf16[2048,512]{1,0:T(8,128)(2,1)} %param.14) | copy-start | bytes 6291460
  245.7 5.6 %copy-start.5 = (bf16[8,256,512]{2,1,0:T(8,128)(2,1)S(1)}, bf16[8,256,512]{2,1,0:T(8,128)(2,1)}, u32[]{:S(2)}) copy-start(bf16[8,256,512]{2,1,0:T(8,128)(2,1)} %get-tuple-element.13) | copy-start | bytes 6291460
  251.4 3.0 copy-start.6
  273.8 6.9 %copy-start.3 = (bf16[4,256,512]{2,1,0:T(8,128)(2,1)S(1)}, bf16[4,256,512]{2,1,0:T(8,128)(2,1)}, u32[]{:S(2)}) copy-start(bf16[4,256,512]{2,1,0:T(8,128)(2,1)} %shard_map.121) | copy-start | bytes 3145732
  298.1 3.0 copy-start.2
  303.5 1.6 copy-start.10
  305.1 1.6 copy-start.11
  306.7 1.6 copy-start.12
  404.8 8.2 %copy-start.7 = (bf16[512,2048]{1,0:T(8,128)(2,1)S(1)}, bf16[512,2048]{1,0:T(8,128)(2,1)}, u32[]{:S(2)}) copy-start(bf16[512,2048]{1,0:T(8,128)(2,1)} %param.20) | copy-start | bytes 6291460
  415.6 15.8 %copy-start.4 = (bf16[256,512]{1,0:T(8,128)(2,1)S(1)}, bf16[256,512]{1,0:T(8,128)(2,1)}, u32[]{:S(2)}) copy-start(bf16[256,512]{1,0:T(8,128)(2,1)} %fusion.13.refs_0_) | copy-start | bytes 786436
  415.6 16.6 %copy-start.1 = (bf16[2048,512]{1,0:T(8,128)(2,1)S(1)}, bf16[2048,512]{1,0:T(8,128)(2,1)}, u32[]{:S(2)}) copy-start(bf16[2048,512]{1,0:T(8,128)(2,1)} %param.13) | copy-start | bytes 6291460
Sparse Core Ops, SparseCore 0:
  10.9 92.2 reduce-scatter.1

commit v2 on v1

--- a/solution.py
+++ b/solution.py
@@ -13,12 +13,6 @@
 log2e = 1.4426950408889634
 MESH = pl.DeviceIdType.MESH
 ANY = pl.BlockSpec(memory_space=pl.ANY)
-
-
-def unpack_bits(packed_words, word_bits):
-    shifts = jnp.arange(word_bits, dtype=jnp.int32)
-    bit_table = jnp.bitwise_and(jnp.right_shift(packed_words[..., None, :], shifts[:, None]), 1)
-    return bit_table.reshape(packed_words.shape[:-1] + (word_bits * packed_words.shape[-1],))
 
 
 def rms_rows(matrix):
@@ -50,9 +44,14 @@
             return ins[a].at[:, pl.ds(start, widths[a])]
         return ins[a]
 
+    def place(a):
+        if modes[a] == "beside":
+            return outs[a].at[:, pl.ds(pl.multiple_of(me * widths[a], 128), widths[a])]
+        return outs[a].at[me]
+
     local = []
     for a in range(count):
-        copy = pltpu.make_async_copy(piece(a, me), outs[a].at[me], local_sem.at[a])
+        copy = pltpu.make_async_copy(piece(a, me), place(a), local_sem.at[a])
         copy.start()
         local.append(copy)
     greet(axis, n, me)
@@ -62,7 +61,7 @@
         for a in range(count):
             copy = pltpu.make_async_remote_copy(
                 src_ref=piece(a, to),
-                dst_ref=outs[a].at[me],
+                dst_ref=place(a),
                 send_sem=send_sem.at[a, d],
                 recv_sem=recv_sem.at[a, d],
                 device_id={axis: to},
@@ -86,7 +85,7 @@
             width = x.shape[1] // n
             shape = (n, x.shape[0], width)
         else:
-            shape, width = (n,) + x.shape, 0
+            shape, width = (x.shape[0], n * x.shape[1]), x.shape[1]
         shapes.append(jax.ShapeDtypeStruct(shape, x.dtype))
         widths.append(width)
     return pl.pallas_call(
@@ -103,83 +102,278 @@
     )(*arrays)
 
 
-def spread_kernel(axis, n, x_ref, out_ref, send_a, recv_a, send_b, recv_b, local_sem):
+def spread_kernel(axis, n, across, chunks, x_ref, out_ref, send_sem, recv_sem, local_sem):
     me = lax.axis_index(axis)
-    root = n - 1
+    down = n // across
+    z, x = me // across, lax.rem(me, across)
+    root = me == n - 1
     greet(axis, n, me)
-
-    def parts(j):
-        return (pl.ds(j * n, n), pl.ds(root * n + j, 1))
-
-    tail = pl.ds(root * n + root, 1)
-
-    def remote(src, dst, send, recv, to):
+    first = x == across - 1
+    top, below = z == down - 1, z == down - 2
+    inner = jnp.logical_and
+    children = (
+        (
+            (inner(first, z > 0), me - across),
+            (inner(jnp.logical_not(top), x > 0), me - 1),
+            (inner(below, jnp.logical_not(first)), me + across),
+        ),
+        (
+            (inner(top, x > 0), me - 1),
+            (inner(x == 0, z > 0), me - across),
+            (inner(jnp.logical_not(top), jnp.logical_not(first)), me + 1),
+        ),
+    )
+
+    def remote(ref, flow, c, child, to):
+        at = flow * chunks + c
         return pltpu.make_async_remote_copy(
-            src_ref=src,
-            dst_ref=dst,
-            send_sem=send,
-            recv_sem=recv,
+            src_ref=ref.at[at],
+            dst_ref=out_ref.at[at],
+            send_sem=send_sem.at[child, at],
+            recv_sem=recv_sem.at[at],
             device_id={axis: to},
             device_id_type=MESH,
         )
 
-    @pl.when(me == root)
+    @pl.when(root)
     def _():
-        copies = []
-        for j in range(root):
-            for p, part in enumerate(parts(j)):
-                copies.append(
-                    remote(x_ref.at[part], out_ref.at[part], send_a.at[p, j], recv_a.at[p], j)
-                )
-                copies[-1].start()
-        for j in range(root):
-            copies.append(
-                remote(x_ref.at[tail], out_ref.at[tail], send_a.at[2, j], recv_a.at[2], j)
-            )
-            copies[-1].start()
         own = pltpu.make_async_copy(x_ref, out_ref, local_sem)
         own.start()
+        copies = []
+        for c in range(chunks):
+            copies.append(remote(x_ref, 0, c, 0, me - across))
+            copies[-1].start()
+            copies.append(remote(x_ref, 1, c, 0, me - 1))
+            copies[-1].start()
         for copy in copies:
             copy.wait_send()
         own.wait()
 
-    @pl.when(me != root)
+    @pl.when(jnp.logical_not(root))
     def _():
-        copies = []
-        for p, part in enumerate(parts(me)):
-            remote(x_ref.at[part], out_ref.at[part], send_a.at[p, 0], recv_a.at[p], root).wait_recv()
-            for d in range(1, root):
-                to = lax.rem(me + d, root)
-                copies.append(
-                    remote(
-                        out_ref.at[part], out_ref.at[part], send_b.at[p, d], recv_b.at[p, d], to
-                    )
-                )
-                copies[-1].start()
-        remote(x_ref.at[tail], out_ref.at[tail], send_a.at[2, 0], recv_a.at[2], root).wait_recv()
-        for copy in copies:
-            copy.wait()
+        for c in range(chunks):
+            for flow in range(2):
+                remote(out_ref, flow, c, 0, n - 1).wait_recv()
+                for child, (there, to) in enumerate(children[flow]):
+
+                    @pl.when(there)
+                    def _():
+                        remote(out_ref, flow, c, child, to).start()
+
+        for flow in range(2):
+            for child, (there, to) in enumerate(children[flow]):
+
+                @pl.when(there)
+                def _():
+                    for c in range(chunks):
+                        remote(out_ref, flow, c, child, to).wait_send()
 
 
 def spread(x, axis, ident):
     n = lax.axis_size(axis)
     rows, width = x.shape
-    grains = x.reshape(n * n, rows // (n * n), width)
+    across = max(d for d in range(1, n) if n % d == 0 and d * d <= n)
+    chunks = 8
+    grains = x.reshape(2 * chunks, rows // (2 * chunks), width)
     out = pl.pallas_call(
-        functools.partial(spread_kernel, axis, n),
+        functools.partial(spread_kernel, axis, n, across, chunks),
         out_shape=jax.ShapeDtypeStruct(grains.shape, x.dtype),
         in_specs=[ANY],
         out_specs=ANY,
         scratch_shapes=[
-            pltpu.SemaphoreType.DMA((3, n)),
-            pltpu.SemaphoreType.DMA((3,)),
-            pltpu.SemaphoreType.DMA((2, n)),
-            pltpu.SemaphoreType.DMA((2, n)),
+            pltpu.SemaphoreType.DMA((3, 2 * chunks)),
+            pltpu.SemaphoreType.DMA((2 * chunks,)),
             pltpu.SemaphoreType.DMA,
         ],
         compiler_params=pltpu.CompilerParams(collective_id=ident, has_side_effects=True),
     )(grains)
     return out.reshape(rows, width)
+
+
+def piece_of(slot, sub, g):
+    return slot * g + (sub if slot % 2 == 0 else g - 1 - sub)
+
+
+def owner_of(me, g):
+    slot, place = me // g, lax.rem(me, g)
+    return slot, jnp.where(lax.rem(slot, 2) == 0, place, g - 1 - place)
+
+
+def deal_kernel(axis, n, heads, hd, *refs):
+    q_ref, k_ref, v_ref, qo, ko, vo, send, recv, qsend, qrecv, local = refs
+    me = lax.axis_index(axis)
+    g = n // heads
+
+    def cut(ref, j):
+        return ref.at[:, pl.ds(pl.multiple_of((j // g) * hd, 128), hd)]
+
+    own = [
+        pltpu.make_async_copy(cut(k_ref, me), ko.at[me], local.at[0]),
+        pltpu.make_async_copy(cut(v_ref, me), vo.at[me], local.at[1]),
+    ]
+    for copy in own:
+        copy.start()
+    slot, sub = owner_of(me, g)
+
+    def query(h):
+        to = h * g + sub
+        return to, pltpu.make_async_remote_copy(
+            src_ref=q_ref.at[:, h * hd : (h + 1) * hd],
+            dst_ref=qo.at[slot],
+            send_sem=qsend.at[h],
+            recv_sem=qrecv.at[slot],
+            device_id={axis: to},
+            device_id_type=MESH,
+        )
+
+    greet(axis, n, me)
+    copies = []
+    for d in range(1, n):
+        to = lax.rem(me + d, n)
+        for a, (ref, out) in enumerate(((k_ref, ko), (v_ref, vo))):
+            copies.append(
+                pltpu.make_async_remote_copy(
+                    src_ref=cut(ref, to),
+                    dst_ref=out.at[me],
+                    send_sem=send.at[a, d],
+                    recv_sem=recv.at[a, d],
+                    device_id={axis: to},
+                    device_id_type=MESH,
+                )
+            )
+            copies[-1].start()
+    for h in range(heads):
+        to, copy = query(h)
+
+        @pl.when(to != me)
+        def _():
+            copy.start()
+
+        @pl.when(to == me)
+        def _():
+            mine = pltpu.make_async_copy(
+                q_ref.at[:, h * hd : (h + 1) * hd], qo.at[slot], local.at[2]
+            )
+            mine.start()
+            mine.wait()
+
+    for copy in copies:
+        copy.wait()
+    for h in range(heads):
+        to, copy = query(h)
+
+        @pl.when(to != me)
+        def _():
+            copy.wait_send()
+
+    for t in range(heads):
+        source = piece_of(t, lax.rem(me, g), g)
+
+        @pl.when(source != me)
+        def _():
+            pltpu.make_async_remote_copy(
+                src_ref=qo.at[t],
+                dst_ref=qo.at[t],
+                send_sem=qsend.at[t],
+                recv_sem=qrecv.at[t],
+                device_id={axis: source},
+                device_id_type=MESH,
+            ).wait_recv()
+
+    for copy in own:
+        copy.wait()
+
+
+def deal(queries, keys, values, axis, hd, ident):
+    n = lax.axis_size(axis)
+    rows, width = queries.shape
+    heads = width // hd
+    whole = jax.ShapeDtypeStruct((n, rows, hd), keys.dtype)
+    return pl.pallas_call(
+        functools.partial(deal_kernel, axis, n, heads, hd),
+        out_shape=(jax.ShapeDtypeStruct((heads, rows, hd), queries.dtype), whole, whole),
+        in_specs=[ANY] * 3,
+        out_specs=(ANY,) * 3,
+        scratch_shapes=[
+            pltpu.SemaphoreType.DMA((2, n)),
+            pltpu.SemaphoreType.DMA((2, n)),
+            pltpu.SemaphoreType.DMA((heads,)),
+            pltpu.SemaphoreType.DMA((heads,)),
+            pltpu.SemaphoreType.DMA((3,)),
+        ],
+        compiler_params=pltpu.CompilerParams(collective_id=ident, has_side_effects=True),
+    )(queries, keys, values)
+
+
+def collect_kernel(axis, n, heads, hd, x_ref, out_ref, send, recv, local):
+    me = lax.axis_index(axis)
+    g = n // heads
+    head = me // g
+    cols = pl.ds(pl.multiple_of(head * hd, 128), hd)
+    greet(axis, n, me)
+
+    def outgoing(t):
+        to = piece_of(t, lax.rem(me, g), g)
+        return to, pltpu.make_async_remote_copy(
+            src_ref=x_ref.at[t],
+            dst_ref=out_ref.at[:, cols],
+            send_sem=send.at[t],
+            recv_sem=recv.at[head],
+            device_id={axis: to},
+            device_id_type=MESH,
+        )
+
+    for t in range(heads):
+        to, copy = outgoing(t)
+
+        @pl.when(to != me)
+        def _():
+            copy.start()
+
+        @pl.when(to == me)
+        def _():
+            mine = pltpu.make_async_copy(x_ref.at[t], out_ref.at[:, cols], local)
+            mine.start()
+            mine.wait()
+
+    for t in range(heads):
+        to, copy = outgoing(t)
+
+        @pl.when(to != me)
+        def _():
+            copy.wait_send()
+
+    slot, sub = owner_of(me, g)
+    for h in range(heads):
+        source = h * g + sub
+
+        @pl.when(source != me)
+        def _():
+            pltpu.make_async_remote_copy(
+                src_ref=x_ref.at[0],
+                dst_ref=out_ref.at[:, h * hd : (h + 1) * hd],
+                send_sem=send.at[0],
+                recv_sem=recv.at[h],
+                device_id={axis: source},
+                device_id_type=MESH,
+            ).wait_recv()
+
+
+def collect(x, axis, ident):
+    n = lax.axis_size(axis)
+    heads, rows, hd = x.shape
+    return pl.pallas_call(
+        functools.partial(collect_kernel, axis, n, heads, hd),
+        out_shape=jax.ShapeDtypeStruct((rows, heads * hd), x.dtype),
+        in_specs=[ANY],
+        out_specs=ANY,
+        scratch_shapes=[
+            pltpu.SemaphoreType.DMA((heads,)),
+            pltpu.SemaphoreType.DMA((heads,)),
+            pltpu.SemaphoreType.DMA,
+        ],
+        compiler_params=pltpu.CompilerParams(collective_id=ident, has_side_effects=True),
+    )(x)
 
 
 def dot_t(a, b):
@@ -304,17 +498,15 @@
     )(queries, keys, values, words)
 
 
-def latent_kernel(hd, scale, q_ref, k_ref, v_ref, w_ref, o_ref, s_ref):
-    rows = q_ref.shape[0]
+def latent_kernel(hd, scale, at_ref, q_ref, k_ref, v_ref, w_ref, o_ref, s_ref):
+    rows = q_ref.shape[1]
     pieces, piece_rows = k_ref.shape[0], k_ref.shape[1]
     chunk = w_ref.shape[2]
     factor = scale * log2e
-    first_row = lax.axis_index("seq") * rows
-    used = first_row + rows
-    row = first_row + lax.broadcasted_iota(jnp.int32, (rows, chunk), 0)
+    row = at_ref[1 + pl.program_id(0)] * rows + lax.broadcasted_iota(jnp.int32, (rows, chunk), 0)
     lane = lax.broadcasted_iota(jnp.int32, (rows, chunk), 1)
     per = piece_rows // chunk
-    q = q_ref[...]
+    q = q_ref[0]
     words = w_ref[0]
     tops = jnp.full((rows, 128), masked, jnp.float32)
     for p in range(pieces):
@@ -338,27 +530,59 @@
         weights = jnp.concatenate(kept, axis=1) if per > 1 else kept[0]
         acc = acc + jnp.dot(weights, v_ref[p], preferred_element_type=jnp.float32)
     total = jnp.sum(sums, axis=1, keepdims=True)
-    o_ref[...] = (acc * (keep_scale / total)).astype(o_ref.dtype)
-
-
-def latent_attention(queries, keys, values, words, hd):
-    rows, width = queries.shape
+    o_ref[0] = (acc * (keep_scale / total)).astype(o_ref.dtype)
+
+
+def latent_attention(places, queries, keys, values, words):
+    slots, rows, hd = queries.shape
     pieces, piece_rows, _ = keys.shape
-    heads = width // hd
     chunk = words.shape[2]
     return pl.pallas_call(
         functools.partial(latent_kernel, hd, 1.0 / math.sqrt(hd)),
-        grid=(heads,),
-        in_specs=[
-            pl.BlockSpec((rows, hd), lambda h: (0, h)),
-            pl.BlockSpec((pieces, piece_rows, hd), lambda h: (0, 0, h)),
-            pl.BlockSpec((pieces, piece_rows, hd), lambda h: (0, 0, h)),
-            pl.BlockSpec((1, rows, chunk), lambda h: (h, 0, 0)),
-        ],
-        out_specs=pl.BlockSpec((rows, hd), lambda h: (0, h)),
-        out_shape=jax.ShapeDtypeStruct((rows, width), jnp.bfloat16),
-        scratch_shapes=[pltpu.VMEM((pieces * piece_rows // chunk, rows, chunk), jnp.float32)],
-    )(queries, keys, values, words)
+        grid_spec=pltpu.PrefetchScalarGridSpec(
+            num_scalar_prefetch=1,
+            grid=(slots,),
+            in_specs=[
+                pl.BlockSpec((1, rows, hd), lambda t, at: (t, 0, 0)),
+                pl.BlockSpec((pieces, piece_rows, hd), lambda t, at: (0, 0, 0)),
+                pl.BlockSpec((pieces, piece_rows, hd), lambda t, at: (0, 0, 0)),
+                pl.BlockSpec((1, rows, chunk), lambda t, at: (at[0], at[1 + t], 0)),
+            ],
+            out_specs=pl.BlockSpec((1, rows, hd), lambda t, at: (t, 0, 0)),
+            scratch_shapes=[
+                pltpu.VMEM((pieces * piece_rows // chunk, rows, chunk), jnp.float32)
+            ],
+        ),
+        out_shape=jax.ShapeDtypeStruct(queries.shape, jnp.bfloat16),
+    )(places, queries, keys, values, words)
+
+
+def combine_kernel(n, heads, hd, stride, p_ref, level_ref, w_ref, o_ref):
+    levels = level_ref[...]
+    parts = []
+    for h in range(heads):
+        mine = [levels[:, s * stride + h : s * stride + h + 1] for s in range(n)]
+        top = functools.reduce(jnp.maximum, mine)
+        shares = [jnp.exp(level - top) for level in mine]
+        total = functools.reduce(jnp.add, shares)
+        acc = None
+        for s in range(n):
+            term = p_ref[s, :, h * hd : (h + 1) * hd].astype(jnp.float32) * shares[s]
+            acc = term if acc is None else acc + term
+        parts.append((acc / total).astype(jnp.bfloat16))
+    attended = jnp.concatenate(parts, axis=1)
+    o_ref[...] = jnp.dot(attended, w_ref[...], preferred_element_type=jnp.float32).astype(
+        jnp.bfloat16
+    )
+
+
+def combine(partials, levels, weight, heads, hd):
+    n, rows, _ = partials.shape
+    stride = levels.shape[1] // n
+    return pl.pallas_call(
+        functools.partial(combine_kernel, n, heads, hd, stride),
+        out_shape=jax.ShapeDtypeStruct((rows, weight.shape[1]), jnp.bfloat16),
+    )(partials, levels, weight)
 
 
 def per_device(
@@ -391,14 +615,15 @@
 
     normed = rms_rows(context)
     own_queries = project(normed[context.shape[0] - latent_count :], wq_cross)
+    queries = spread(own_queries, "seq", 1)
     own_columns = lax.dynamic_slice_in_dim(
         context[context.shape[0] - latent_count :], head_index * columns, columns, 1
     )
     own_columns = jnp.where(seq_index == seq_count - 1, own_columns, 0).astype(jnp.bfloat16)
+    own_columns, queries = lax.optimization_barrier((own_columns, queries))
     inputs = lax.psum_scatter(own_columns, "seq", scatter_dimension=0, tiled=True)
     key_rows = project(normed, wk_cross)
     value_rows = project(normed, wv_cross)
-    queries = spread(own_queries, "seq", 1)
     partial, stats = cross_attention(
         queries, key_rows, value_rows, cross_keep, seq_count, head_dim
     )
@@ -409,40 +634,33 @@
         "seq",
         2,
     )
-    levels = levels[:, :head_local, :]
-    level_top = jnp.max(levels, axis=0, keepdims=True)
-    share = jnp.exp(levels - level_top)
-    share = share / jnp.sum(share, axis=0, keepdims=True)
-    share = share.transpose(0, 2, 1)[..., None]
-    spread_heads = partials.reshape(seq_count, local_rows, head_local, head_dim)
-    attended = (
-        jnp.sum(spread_heads.astype(jnp.float32) * share, axis=0)
-        .reshape(local_rows, head_local * head_dim)
-        .astype(jnp.bfloat16)
-    )
-    residual_rows = lax.dynamic_slice_in_dim(residual_keep, first_row, local_rows, 1)
-    residual_mask = lax.dynamic_slice_in_dim(
-        unpack_bits(residual_rows, 16), head_index * columns, columns, 2
+    levels = levels.reshape(seq_count * 8, local_rows).T
+    own_branch = combine(partials, levels, wo_cross, head_local, head_dim)
+    branches = exchange([own_branch], ["cols"], "head", 3)[0]
+    words = lax.dynamic_slice_in_dim(residual_keep, first_row, local_rows, 1)
+    blocks = columns // words.shape[2]
+    flags = jnp.concatenate(
+        [jnp.right_shift(words, head_index * blocks + b) & 1 for b in range(blocks)], axis=2
     ).astype(jnp.float32)
-    branches = exchange([project(attended, wo_cross)], ["cols"], "head", 3)[0]
     branch = jnp.sum(branches.astype(jnp.float32), axis=0)
-    latents = (
-        inputs.astype(jnp.float32) + residual_mask[0] * keep_scale * branch
-    ).astype(jnp.bfloat16)
-    gathered = exchange([latents], ["all"], "head", 4)[0]
-    whole_latents = gathered.transpose(1, 0, 2).reshape(local_rows, model_width)
-    normed_latents = rms_rows(whole_latents)
+    latents = (inputs.astype(jnp.float32) + flags[0] * keep_scale * branch).astype(jnp.bfloat16)
+    normed_latents = rms_rows(exchange([latents], ["beside"], "head", 4)[0])
     latent_queries = project(normed_latents, wq_latent)
     latent_keys = project(normed_latents, wk_latent)
     latent_values = project(normed_latents, wv_latent)
-    latent_words = lax.dynamic_slice_in_dim(latent_keep, first_row, local_rows, 1)
-    all_keys, all_values = exchange([latent_keys, latent_values], ["all", "all"], "seq", 5)
-    latent_attended = latent_attention(
-        latent_queries, all_keys, all_values, latent_words, head_dim
-    )
+    dealt_queries, dealt_keys, dealt_values = deal(
+        latent_queries, latent_keys, latent_values, "seq", head_dim, 5
+    )
+    group = seq_count // head_local
+    places = jnp.stack(
+        [seq_index // group]
+        + [piece_of(t, lax.rem(seq_index, group), group) for t in range(head_local)]
+    ).astype(jnp.int32)
+    dealt_out = latent_attention(places, dealt_queries, dealt_keys, dealt_values, latent_keep)
+    latent_attended = collect(dealt_out, "seq", 7)
     latent_branches = exchange([project(latent_attended, wo_latent)], ["cols"], "head", 6)[0]
     latent_branch = jnp.sum(latent_branches.astype(jnp.float32), axis=0)
-    return (latents.astype(jnp.float32) + residual_mask[1] * keep_scale * latent_branch).astype(
+    return (latents.astype(jnp.float32) + flags[1] * keep_scale * latent_branch).astype(
         jnp.bfloat16
     )
 

time: 440 us -> 402 us (0.914)
  local copies, waits for them, and re-layouts: 26 us -> 7.21 us
  Pallas kernels: 339 us -> 330 us
  other arithmetic: 23.2 us -> 15.4 us
    pallas_call x5 -> x4, Pallas kernels: 192 us -> 106 us  [exchange(): pl.pallas_call(functools.partial(exchange_kernel, axis, n, tuple(modes),...]
    pallas_call x1 -> x4, Pallas kernels: 96.9 us -> 172 us  [the longest x1 123 us: spread(): pl.pallas_call(functools.partial(spread_kernel, axis, n, across, chunks),...]
    mul x2 -> x0, local copies, waits for them, and re-layouts: 9.44 us -> none  [per_device(): spread_heads.astype(jnp.float32) * share]
    shift_right_arithmetic x3 -> x0, local copies, waits for them, and re-layouts: 7.21 us -> none  [unpack_bits(): jnp.right_shift(packed_words[..., None, :], shifts[:, None])]
    convert_element_type x5 -> x3, other arithmetic: 7.15 us -> 2.7 us  [the longest x1 1.79 us: per_device(): (inputs.astype(jnp.float32) + flags[0] * keep_scale * branch).astype(jnp....]
    dot_general x8 -> x7, matrix products: 37.3 us -> 34 us  [project(): jnp.dot(rows, weight, preferred_element_type=jnp.float32)]
  transfers between devices with their start and end apart: 1 -> 1, of which waited for: 0 -> 0; matrix products, arithmetic and copies ran while one was open for 15% -> 6% of each run, Pallas kernels for 47% -> 31%
where the time goes in v2:
time: 402 us; the launch traced here: 400 us
  Pallas kernels  330 us (82%)
  matrix products  34 us (8%)
  other arithmetic  15.4 us (4%)
  between operations  13.6 us (3%)
  local copies, waits for them, and re-layouts  7.21 us (2%)
    pallas_call x1, Pallas kernels, spread(): pl.pallas_call(functools.partial(spread_kernel, axis, n, across, chunks),...  123 us
    pallas_call x4, Pallas kernels, exchange(): pl.pallas_call(functools.partial(exchange_kernel, axis, n, tuple(modes),...  106 us
    pallas_call x1, Pallas kernels, cross_attention(): pl.pallas_call(functools.partial(cross_kernel, n, hd, 1.0 / math.sqrt(hd)...  42.1 us
    dot_general x7, matrix products, project(): jnp.dot(rows, weight, preferred_element_type=jnp.float32)  34 us
    pallas_call x1, Pallas kernels, deal(): pl.pallas_call(functools.partial(deal_kernel, axis, n, heads, hd), out_sh...  31.4 us
    pallas_call x1, Pallas kernels, collect(): pl.pallas_call(functools.partial(collect_kernel, axis, n, heads, hd), out...  11.8 us
    pallas_call x1, Pallas kernels, latent_attention(): pl.pallas_call(functools.partial(latent_kernel, hd, 1.0 / math.sqrt(hd)),...  8.84 us
  transfers between devices with their start and end apart: 1, of which 0 were waited for; matrix products, arithmetic and copies ran while one was open for 6% of the time, Pallas kernels for 31%

profile of v2, /device:TPU:11, one launch (start us, length us, event | category | flops | bytes accessed | tf_op | source)
XLA Modules:
  0.0 399.8 jit_solution(6893138312989046197)
XLA Ops:
  6.5 5.2 %fusion = f32[2048]{0:T(1024)S(1)} fusion(bf16[2048,2048]{1,0:T(8,128)(2,1)} %param.12), kind=kLoop, calls=%fused_computation.2 | loop fusion | flops 12580864 | bytes 8396800 | tf_op jit(solution)/shard_map/reduce_sum | solution.py:20
  12.9 5.8 %convolution_convert_fusion.2 = bf16[2048,512]{1,0:T(8,128)(2,1)} fusion(bf16[2048,512]{1,0:T(8,128)(2,1)S(1)} %copy-done, bf16[2048,2048]{1,0:T(8,128)(2,1)S(1)} %copy-done.2, f32[2048]{0:T(1024)S(1)} %add_rsqrt_fusion), kind=kOutput, calls=%fused_computation.6 | convolution fusion | flops 4308598784 | bytes 12591104 | tf_op jit(solution)/shard_map/dot_general | solution.py:614
  18.8 122.9 %shard_map.118 = bf16[16,128,512]{2,1,0:T(8,128)(2,1)} custom-call(bf16[16,128,512]{2,1,0:T(8,128)(2,1)} %bitcast.40), custom_call_target="tpu_custom_call" | custom-call | tf_op jit(solution)/shard_map/pallas_call | solution.py:178
  141.7 3.3 dynamic-slice_select_fusion
  145.0 1.6 copy-done.7
  146.6 9.6 %convolution_convert_fusion.1.k_ref = bf16[2048,512]{1,0:T(8,128)(2,1)} fusion(bf16[2048,512]{1,0:T(8,128)(2,1)S(1)} %copy-done.7, bf16[2048,2048]{1,0:T(8,128)(2,1)} %param.12, f32[2048]{0:T(1024)S(1)} %add_rsqrt_fusion), kind=kOutput, calls=%fused_computation.5 | convolution fusion | flops 4308598784 | bytes 12591104 | tf_op jit(solution)/shard_map/dot_general | solution.py:614
  156.2 9.5 %convolution_convert_fusion.v_ref = bf16[2048,512]{1,0:T(8,128)(2,1)} fusion(bf16[2048,512]{1,0:T(8,128)(2,1)S(1)} %copy-done.8, bf16[2048,2048]{1,0:T(8,128)(2,1)} %param.12, f32[2048]{0:T(1024)S(1)} %add_rsqrt_fusion), kind=kOutput, calls=%fused_computation.4 | convolution fusion | flops 4308598784 | bytes 12591104 | tf_op jit(solution)/shard_map/dot_general | solution.py:614
  165.7 42.1 %shard_map.119 = (bf16[2048,512]{1,0:T(8,128)(2,1)}, f32[2048,128]{1,0:T(8,128)}) custom-call(bf16[2048,512]{1,0:T(8,128)(2,1)} %bitcast.38, bf16[2048,512]{1,0:T(8,128)(2,1)} %convolution_convert_fusion.1.k_ref, bf16[2048,512]{1,0:T(8,128)(2,1)} %convolution_convert_fusion.v_ref, s32[4,2048,256]{2,1,0:T(8,128)} %w_ref.3), custom_call_target="tpu_custom_call" | custom-call | flops 34359738368 | bytes 8388608 | tf_op jit(solution)/shard_map/pallas_call | solution.py:475
  207.9 2.2 copy.14
  210.0 51.5 %shard_map.120 = (bf16[8,256,512]{2,1,0:T(8,128)(2,1)}, f32[8,8,256]{2,1,0:T(8,128)}) custom-call(bf16[8,256,512]{2,1,0:T(8,128)(2,1)} %bitcast.39, f32[8,8,256]{2,1,0:T(8,128)} %bitcast.43), custom_call_target="tpu_custom_call" | custom-call | tf_op jit(solution)/shard_map/pallas_call | solution.py:91
  261.6 1.6 copy.15
  263.1 6.2 %shard_map.121.refs_0_ = bf16[256,2048]{1,0:T(8,128)(2,1)} custom-call(bf16[8,256,512]{2,1,0:T(8,128)(2,1)} %get-tuple-element.18.p_ref, f32[256,64]{1,0:T(8,128)} %bitcast.42, bf16[512,2048]{1,0:T(8,128)(2,1)} %w_ref.4), custom_call_target="tpu_custom_call" | custom-call | tf_op jit(solution)/shard_map/pallas_call | solution.py:582
  269.4 25.7 %shard_map.122 = bf16[4,256,512]{2,1,0:T(8,128)(2,1)} custom-call(bf16[256,2048]{1,0:T(8,128)(2,1)} %shard_map.121.refs_0_), custom_call_target="tpu_custom_call" | custom-call | tf_op jit(solution)/shard_map/pallas_call | solution.py:91
  297.0 1.8 fusion.11.refs_0_
  298.7 14.0 %shard_map.123 = bf16[256,2048]{1,0:T(8,128)(2,1)} custom-call(bf16[256,512]{1,0:T(8,128)(2,1)} %fusion.11.refs_0_), custom_call_target="tpu_custom_call" | custom-call | tf_op jit(solution)/shard_map/pallas_call | solution.py:91
  312.8 1.5 fusion.2
  314.3 3.5 convolution_convert_fusion.6.refs_0_
  317.9 1.5 convolution_convert_fusion.5.refs_1_
  319.5 1.5 convolution_convert_fusion.4.refs_2_
  320.9 31.4 %shard_map.124 = (bf16[4,256,128]{2,1,0:T(8,128)(2,1)}, bf16[8,256,128]{2,1,0:T(8,128)(2,1)}, bf16[8,256,128]{2,1,0:T(8,128)(2,1)}) custom-call(bf16[256,512]{1,0:T(8,128)(2,1)} %convolution_convert_fusion.6.refs_0_, bf16[256,512]{1,0:T(8,128)(2,1)} %convolution_convert_fusion.5.refs_1_, bf16[256,512]{1,0:T(8,128)(2,1)} %convolution_convert_fusion.4.refs_2_), custom_call_target="tpu_custom_call" | custom-call | tf_op jit(solution)/shard_map/pallas_call | solution.py:292
  352.3 8.8 %shard_map.125.x_ref = bf16[4,256,128]{2,1,0:T(8,128)(2,1)} custom-call(s32[5]{0:T(128)} %stack.23.at_ref, bf16[4,256,128]{2,1,0:T(8,128)(2,1)} %get-tuple-element.20.q_ref, bf16[8,256,128]{2,1,0:T(8,128)(2,1)} %get-tuple-element.21.k_ref, bf16[8,256,128]{2,1,0:T(8,128)(2,1)} %get-tuple-element.22.v_ref, s32[4,2048,128]{2,1,0:T(8,128)} %w_ref.5), custom_call_target="tpu_custom_call" | custom-call | tf_op jit(solution)/shard_map/pallas_call | solution.py:540
  361.2 11.8 %shard_map.126 = bf16[256,512]{1,0:T(8,128)(2,1)} custom-call(bf16[4,256,128]{2,1,0:T(8,128)(2,1)} %shard_map.125.x_ref), custom_call_target="tpu_custom_call" | custom-call | tf_op jit(solution)/shard_map/pallas_call | solution.py:365
  373.0 2.6 convolution_convert_fusion.3.refs_0_
  375.6 15.0 %shard_map.127 = bf16[4,256,512]{2,1,0:T(8,128)(2,1)} custom-call(bf16[256,2048]{1,0:T(8,128)(2,1)} %convolution_convert_fusion.3.refs_0_), custom_call_target="tpu_custom_call" | custom-call | tf_op jit(solution)/shard_map/pallas_call | solution.py:91
  (32 shorter events, 5.5 us)
Async XLA Ops:
  6.5 5.3 %copy-start = (bf16[2048,512]{1,0:T(8,128)(2,1)S(1)}, bf16[2048,512]{1,0:T(8,128)(2,1)}, u32[]{:S(2)}) copy-start(bf16[2048,512]{1,0:T(8,128)(2,1)} %param.13) | copy-start | bytes 6291460
  6.5 290.4 %reduce-scatter.2.cloned.1.call-start = ((), (), s32[]{:S(2)}) async-start(), calls=%async_computation.1 | async-start | bytes 2359296 | tf_op jit(solution)/shard_map/reduce_scatter | solution.py:624
  6.5 6.4 %copy-start.2 = (bf16[2048,2048]{1,0:T(8,128)(2,1)S(1)}, bf16[2048,2048]{1,0:T(8,128)(2,1)}, u32[]{:S(2)}) copy-start(bf16[2048,2048]{1,0:T(8,128)(2,1)} %param.12) | copy-start | bytes 25165828
  145.0 1.6 copy-start.7
  146.6 9.6 %copy-start.8 = (bf16[2048,512]{1,0:T(8,128)(2,1)S(1)}, bf16[2048,512]{1,0:T(8,128)(2,1)}, u32[]{:S(2)}) copy-start(bf16[2048,512]{1,0:T(8,128)(2,1)} %param.15) | copy-start | bytes 6291460
  295.1 1.7 copy-start.4
  314.3 3.6 copy-start.3
  314.3 3.6 copy-start.9
  317.9 1.6 copy-start.10
  352.3 20.7 %copy-start.6 = (bf16[512,2048]{1,0:T(8,128)(2,1)S(1)}, bf16[512,2048]{1,0:T(8,128)(2,1)}, u32[]{:S(2)}) copy-start(bf16[512,2048]{1,0:T(8,128)(2,1)} %param.20) | copy-start | bytes 6291460
  375.6 16.5 %copy-start.5 = (bf16[256,512]{1,0:T(8,128)(2,1)S(1)}, bf16[256,512]{1,0:T(8,128)(2,1)}, u32[]{:S(2)}) copy-start(bf16[256,512]{1,0:T(8,128)(2,1)} %fusion.11.refs_0_) | copy-start | bytes 786436
  375.6 17.3 %copy-start.1 = (bf16[2048,512]{1,0:T(8,128)(2,1)S(1)}, bf16[2048,512]{1,0:T(8,128)(2,1)}, u32[]{:S(2)}) copy-start(bf16[2048,512]{1,0:T(8,128)(2,1)} %param.13) | copy-start | bytes 6291460
Sparse Core Ops, SparseCore 0:
  145.1 103.1 reduce-scatter.1

commit v3 on v2

--- a/solution.py
+++ b/solution.py
@@ -30,10 +30,20 @@
     pl.semaphore_wait(barrier, n - 1)
 
 
+def relay(src, buffer, dst, sem):
+    inward = pltpu.make_async_copy(src, buffer, sem)
+    inward.start()
+    inward.wait()
+    outward = pltpu.make_async_copy(buffer, dst, sem)
+    outward.start()
+    return outward
+
+
 def exchange_kernel(axis, n, modes, widths, *refs):
     count = len(modes)
     ins, outs = refs[:count], refs[count : 2 * count]
-    send_sem, recv_sem, local_sem = refs[2 * count :]
+    send_sem, recv_sem, local_sem = refs[2 * count : 2 * count + 3]
+    buffers = refs[2 * count + 3 :]
     me = lax.axis_index(axis)
 
     def piece(a, j):
@@ -49,11 +59,6 @@
             return outs[a].at[:, pl.ds(pl.multiple_of(me * widths[a], 128), widths[a])]
         return outs[a].at[me]
 
-    local = []
-    for a in range(count):
-        copy = pltpu.make_async_copy(piece(a, me), place(a), local_sem.at[a])
-        copy.start()
-        local.append(copy)
     greet(axis, n, me)
     copies = []
     for d in range(1, n):
@@ -69,25 +74,29 @@
             )
             copy.start()
             copies.append(copy)
+    for a in range(count):
+        copies.append(relay(piece(a, me), buffers[a], place(a), local_sem.at[a]))
     for copy in copies:
         copy.wait()
-    for copy in local:
-        copy.wait()
 
 
 def exchange(arrays, modes, axis, ident):
     n = lax.axis_size(axis)
-    shapes, widths = [], []
+    shapes, widths, buffers = [], [], []
     for x, mode in zip(arrays, modes):
         if mode == "lead":
             shape, width = x.shape, 0
+            own = x.shape[1:]
         elif mode == "cols":
             width = x.shape[1] // n
             shape = (n, x.shape[0], width)
+            own = shape[1:]
         else:
             shape, width = (x.shape[0], n * x.shape[1]), x.shape[1]
+            own = x.shape
         shapes.append(jax.ShapeDtypeStruct(shape, x.dtype))
         widths.append(width)
+        buffers.append(pltpu.VMEM(own, x.dtype))
     return pl.pallas_call(
         functools.partial(exchange_kernel, axis, n, tuple(modes), tuple(widths)),
         out_shape=tuple(shapes),
@@ -97,12 +106,13 @@
             pltpu.SemaphoreType.DMA((len(arrays), n)),
             pltpu.SemaphoreType.DMA((len(arrays), n)),
             pltpu.SemaphoreType.DMA((len(arrays),)),
-        ],
+        ]
+        + buffers,
         compiler_params=pltpu.CompilerParams(collective_id=ident, has_side_effects=True),
     )(*arrays)
 
 
-def spread_kernel(axis, n, across, chunks, x_ref, out_ref, send_sem, recv_sem, local_sem):
+def spread_kernel(axis, n, across, chunks, x_ref, out_ref, send_sem, recv_sem):
     me = lax.axis_index(axis)
     down = n // across
     z, x = me // across, lax.rem(me, across)
@@ -137,17 +147,14 @@
 
     @pl.when(root)
     def _():
-        own = pltpu.make_async_copy(x_ref, out_ref, local_sem)
-        own.start()
         copies = []
         for c in range(chunks):
-            copies.append(remote(x_ref, 0, c, 0, me - across))
+            copies.append(remote(out_ref, 0, c, 0, me - across))
             copies[-1].start()
-            copies.append(remote(x_ref, 1, c, 0, me - 1))
+            copies.append(remote(out_ref, 1, c, 0, me - 1))
             copies[-1].start()
         for copy in copies:
             copy.wait_send()
-        own.wait()
 
     @pl.when(jnp.logical_not(root))
     def _():
@@ -173,17 +180,17 @@
     n = lax.axis_size(axis)
     rows, width = x.shape
     across = max(d for d in range(1, n) if n % d == 0 and d * d <= n)
-    chunks = 8
+    chunks = 16
     grains = x.reshape(2 * chunks, rows // (2 * chunks), width)
     out = pl.pallas_call(
         functools.partial(spread_kernel, axis, n, across, chunks),
         out_shape=jax.ShapeDtypeStruct(grains.shape, x.dtype),
         in_specs=[ANY],
         out_specs=ANY,
+        input_output_aliases={0: 0},
         scratch_shapes=[
             pltpu.SemaphoreType.DMA((3, 2 * chunks)),
             pltpu.SemaphoreType.DMA((2 * chunks,)),
-            pltpu.SemaphoreType.DMA,
         ],
         compiler_params=pltpu.CompilerParams(collective_id=ident, has_side_effects=True),
     )(grains)
@@ -200,19 +207,13 @@
 
 
 def deal_kernel(axis, n, heads, hd, *refs):
-    q_ref, k_ref, v_ref, qo, ko, vo, send, recv, qsend, qrecv, local = refs
+    q_ref, k_ref, v_ref, qo, ko, vo, send, recv, qsend, qrecv, local, buffer = refs
     me = lax.axis_index(axis)
     g = n // heads
 
     def cut(ref, j):
         return ref.at[:, pl.ds(pl.multiple_of((j // g) * hd, 128), hd)]
 
-    own = [
-        pltpu.make_async_copy(cut(k_ref, me), ko.at[me], local.at[0]),
-        pltpu.make_async_copy(cut(v_ref, me), vo.at[me], local.at[1]),
-    ]
-    for copy in own:
-        copy.start()
     slot, sub = owner_of(me, g)
 
     def query(h):
@@ -251,12 +252,12 @@
 
         @pl.when(to == me)
         def _():
-            mine = pltpu.make_async_copy(
-                q_ref.at[:, h * hd : (h + 1) * hd], qo.at[slot], local.at[2]
-            )
-            mine.start()
-            mine.wait()
-
+            relay(
+                q_ref.at[:, h * hd : (h + 1) * hd], buffer.at[2], qo.at[slot], local.at[2]
+            ).wait()
+
+    copies.append(relay(cut(k_ref, me), buffer.at[0], ko.at[me], local.at[0]))
+    copies.append(relay(cut(v_ref, me), buffer.at[1], vo.at[me], local.at[1]))
     for copy in copies:
         copy.wait()
     for h in range(heads):
@@ -279,9 +280,6 @@
                 device_id={axis: source},
                 device_id_type=MESH,
             ).wait_recv()
-
-    for copy in own:
-        copy.wait()
 
 
 def deal(queries, keys, values, axis, hd, ident):
@@ -300,12 +298,13 @@
             pltpu.SemaphoreType.DMA((heads,)),
             pltpu.SemaphoreType.DMA((heads,)),
             pltpu.SemaphoreType.DMA((3,)),
+            pltpu.VMEM((3, rows, hd), keys.dtype),
         ],
         compiler_params=pltpu.CompilerParams(collective_id=ident, has_side_effects=True),
     )(queries, keys, values)
 
 
-def collect_kernel(axis, n, heads, hd, x_ref, out_ref, send, recv, local):
+def collect_kernel(axis, n, heads, hd, x_ref, out_ref, send, recv, local, buffer):
     me = lax.axis_index(axis)
     g = n // heads
     head = me // g
@@ -332,9 +331,7 @@
 
         @pl.when(to == me)
         def _():
-            mine = pltpu.make_async_copy(x_ref.at[t], out_ref.at[:, cols], local)
-            mine.start()
-            mine.wait()
+            relay(x_ref.at[t], buffer, out_ref.at[:, cols], local).wait()
 
     for t in range(heads):
         to, copy = outgoing(t)
@@ -371,6 +368,7 @@
             pltpu.SemaphoreType.DMA((heads,)),
             pltpu.SemaphoreType.DMA((heads,)),
             pltpu.SemaphoreType.DMA,
+            pltpu.VMEM((rows, hd), x.dtype),
         ],
         compiler_params=pltpu.CompilerParams(collective_id=ident, has_side_effects=True),
     )(x)

time: 402 us -> 498 us (1.24)
  Pallas kernels: 330 us -> 426 us
    pallas_call x1, Pallas kernels: 123 us -> 186 us  [spread(): pl.pallas_call(functools.partial(spread_kernel, axis, n, across, chunks),...]
    pallas_call x4, Pallas kernels: 106 us -> 140 us  [exchange(): pl.pallas_call(functools.partial(exchange_kernel, axis, n, tuple(modes),...]
  transfers between devices with their start and end apart: 1 -> 1, of which waited for: 0 -> 0; matrix products, arithmetic and copies ran while one was open for 6% -> 5% of each run, Pallas kernels for 31% -> 32%
where the time goes in v3:
time: 498 us; the launch traced here: 497 us
  Pallas kernels  426 us (86%)
  matrix products  35.3 us (7%)
  other arithmetic  16.4 us (3%)
  between operations  13.5 us (3%)
  local copies, waits for them, and re-layouts  5.76 us (1%)
    pallas_call x1, Pallas kernels, spread(): pl.pallas_call(functools.partial(spread_kernel, axis, n, across, chunks),...  186 us
    pallas_call x4, Pallas kernels, exchange(): pl.pallas_call(functools.partial(exchange_kernel, axis, n, tuple(modes),...  140 us
    pallas_call x1, Pallas kernels, cross_attention(): pl.pallas_call(functools.partial(cross_kernel, n, hd, 1.0 / math.sqrt(hd)...  42.2 us
    dot_general x7, matrix products, project(): jnp.dot(rows, weight, preferred_element_type=jnp.float32)  35.3 us
    pallas_call x1, Pallas kernels, deal(): pl.pallas_call(functools.partial(deal_kernel, axis, n, heads, hd), out_sh...  31.5 us
    pallas_call x1, Pallas kernels, collect(): pl.pallas_call(functools.partial(collect_kernel, axis, n, heads, hd), out...  11.3 us
  transfers between devices with their start and end apart: 1, of which 0 were waited for; matrix products, arithmetic and copies ran while one was open for 5% of the time, Pallas kernels for 32%

profile of v3, /device:TPU:11, one launch (start us, length us, event | category | flops | bytes accessed | tf_op | source)
XLA Modules:
  0.0 496.8 jit_solution(15962098220542345754)
XLA Ops:
  6.5 5.2 %fusion = f32[2048]{0:T(1024)S(1)} fusion(bf16[2048,2048]{1,0:T(8,128)(2,1)} %param.12), kind=kLoop, calls=%fused_computation.2 | loop fusion | flops 12580864 | bytes 8396800 | tf_op jit(solution)/shard_map/reduce_sum | solution.py:20
  12.9 5.8 %convolution_convert_fusion.2 = bf16[2048,512]{1,0:T(8,128)(2,1)} fusion(bf16[2048,512]{1,0:T(8,128)(2,1)S(1)} %copy-done, bf16[2048,2048]{1,0:T(8,128)(2,1)S(1)} %copy-done.1, f32[2048]{0:T(1024)S(1)} %add_rsqrt_fusion), kind=kOutput, calls=%fused_computation.6 | convolution fusion | flops 4308598784 | bytes 12591104 | tf_op jit(solution)/shard_map/dot_general | solution.py:612
  18.7 185.8 %shard_map.118 = bf16[32,64,512]{2,1,0:T(8,128)(2,1)} custom-call(bf16[32,64,512]{2,1,0:T(8,128)(2,1)} %bitcast.39), custom_call_target="tpu_custom_call", output_to_operand_aliasing={{}: (0, {})} | custom-call | tf_op jit(solution)/shard_map/pallas_call | solution.py:185
  204.5 3.3 dynamic-slice_select_fusion
  207.8 10.2 %convolution_convert_fusion.1.k_ref = bf16[2048,512]{1,0:T(8,128)(2,1)} fusion(bf16[2048,512]{1,0:T(8,128)(2,1)} %param.14, bf16[2048,2048]{1,0:T(8,128)(2,1)} %param.12, f32[2048]{0:T(1024)S(1)} %add_rsqrt_fusion), kind=kOutput, calls=%fused_computation.5 | convolution fusion | flops 4308598784 | bytes 12591104 | tf_op jit(solution)/shard_map/dot_general | solution.py:612
  218.1 9.5 %convolution_convert_fusion.v_ref = bf16[2048,512]{1,0:T(8,128)(2,1)} fusion(bf16[2048,512]{1,0:T(8,128)(2,1)S(1)} %copy-done.5, bf16[2048,2048]{1,0:T(8,128)(2,1)} %param.12, f32[2048]{0:T(1024)S(1)} %add_rsqrt_fusion), kind=kOutput, calls=%fused_computation.4 | convolution fusion | flops 4308598784 | bytes 12591104 | tf_op jit(solution)/shard_map/dot_general | solution.py:612
  227.6 42.2 %shard_map.119 = (bf16[2048,512]{1,0:T(8,128)(2,1)}, f32[2048,128]{1,0:T(8,128)}) custom-call(bf16[2048,512]{1,0:T(8,128)(2,1)} %bitcast.40, bf16[2048,512]{1,0:T(8,128)(2,1)} %convolution_convert_fusion.1.k_ref, bf16[2048,512]{1,0:T(8,128)(2,1)} %convolution_convert_fusion.v_ref, s32[4,2048,256]{2,1,0:T(8,128)} %w_ref.3), custom_call_target="tpu_custom_call" | custom-call | flops 34359738368 | bytes 8388608 | tf_op jit(solution)/shard_map/pallas_call | solution.py:473
  269.7 2.2 copy.15
  271.9 44.6 %shard_map.120 = (bf16[8,256,512]{2,1,0:T(8,128)(2,1)}, f32[8,8,256]{2,1,0:T(8,128)}) custom-call(bf16[8,256,512]{2,1,0:T(8,128)(2,1)} %bitcast.38, f32[8,8,256]{2,1,0:T(8,128)} %bitcast.43), custom_call_target="tpu_custom_call" | custom-call | tf_op jit(solution)/shard_map/pallas_call | solution.py:100
  316.5 1.6 copy.16
  318.1 6.3 %shard_map.121.refs_0_ = bf16[256,2048]{1,0:T(8,128)(2,1)} custom-call(bf16[8,256,512]{2,1,0:T(8,128)(2,1)} %get-tuple-element.18.p_ref, f32[256,64]{1,0:T(8,128)} %bitcast.42, bf16[512,2048]{1,0:T(8,128)(2,1)} %w_ref.4), custom_call_target="tpu_custom_call" | custom-call | tf_op jit(solution)/shard_map/pallas_call | solution.py:580
  324.3 66.9 %shard_map.122 = bf16[4,256,512]{2,1,0:T(8,128)(2,1)} custom-call(bf16[256,2048]{1,0:T(8,128)(2,1)} %shard_map.121.refs_0_), custom_call_target="tpu_custom_call" | custom-call | tf_op jit(solution)/shard_map/pallas_call | solution.py:100
  394.1 1.9 fusion.11.refs_0_
  396.0 14.0 %shard_map.123 = bf16[256,2048]{1,0:T(8,128)(2,1)} custom-call(bf16[256,512]{1,0:T(8,128)(2,1)} %fusion.11.refs_0_), custom_call_target="tpu_custom_call" | custom-call | tf_op jit(solution)/shard_map/pallas_call | solution.py:100
  410.1 1.5 fusion.2
  411.6 3.5 convolution_convert_fusion.6.refs_0_
  415.2 1.5 convolution_convert_fusion.5.refs_1_
  416.8 1.5 convolution_convert_fusion.4.refs_2_
  418.2 31.5 %shard_map.124 = (bf16[4,256,128]{2,1,0:T(8,128)(2,1)}, bf16[8,256,128]{2,1,0:T(8,128)(2,1)}, bf16[8,256,128]{2,1,0:T(8,128)(2,1)}) custom-call(bf16[256,512]{1,0:T(8,128)(2,1)} %convolution_convert_fusion.6.refs_0_, bf16[256,512]{1,0:T(8,128)(2,1)} %convolution_convert_fusion.5.refs_1_, bf16[256,512]{1,0:T(8,128)(2,1)} %convolution_convert_fusion.4.refs_2_), custom_call_target="tpu_custom_call" | custom-call | tf_op jit(solution)/shard_map/pallas_call | solution.py:290
  449.7 8.7 %shard_map.125.x_ref = bf16[4,256,128]{2,1,0:T(8,128)(2,1)} custom-call(s32[5]{0:T(128)} %stack.23.at_ref, bf16[4,256,128]{2,1,0:T(8,128)(2,1)} %get-tuple-element.20.q_ref, bf16[8,256,128]{2,1,0:T(8,128)(2,1)} %get-tuple-element.21.k_ref, bf16[8,256,128]{2,1,0:T(8,128)(2,1)} %get-tuple-element.22.v_ref, s32[4,2048,128]{2,1,0:T(8,128)} %w_ref.5), custom_call_target="tpu_custom_call" | custom-call | tf_op jit(solution)/shard_map/pallas_call | solution.py:538
  458.4 11.3 %shard_map.126 = bf16[256,512]{1,0:T(8,128)(2,1)} custom-call(bf16[4,256,128]{2,1,0:T(8,128)(2,1)} %shard_map.125.x_ref), custom_call_target="tpu_custom_call" | custom-call | tf_op jit(solution)/shard_map/pallas_call | solution.py:362
  469.7 3.4 convolution_convert_fusion.3.refs_0_
  473.1 14.6 %shard_map.127 = bf16[4,256,512]{2,1,0:T(8,128)(2,1)} custom-call(bf16[256,2048]{1,0:T(8,128)(2,1)} %convolution_convert_fusion.3.refs_0_), custom_call_target="tpu_custom_call" | custom-call | tf_op jit(solution)/shard_map/pallas_call | solution.py:100
  487.7 1.4 convert_reduce_fusion
  (26 shorter events, 5.0 us)
Async XLA Ops:
  6.5 5.3 %copy-start = (bf16[2048,512]{1,0:T(8,128)(2,1)S(1)}, bf16[2048,512]{1,0:T(8,128)(2,1)}, u32[]{:S(2)}) copy-start(bf16[2048,512]{1,0:T(8,128)(2,1)} %param.13) | copy-start | bytes 6291460
  6.5 387.6 %reduce-scatter.2.cloned.1.call-start = ((), (), s32[]{:S(2)}) async-start(), calls=%async_computation.1 | async-start | bytes 2359296 | tf_op jit(solution)/shard_map/reduce_scatter | solution.py:622
  6.5 6.4 %copy-start.1 = (bf16[2048,2048]{1,0:T(8,128)(2,1)S(1)}, bf16[2048,2048]{1,0:T(8,128)(2,1)}, u32[]{:S(2)}) copy-start(bf16[2048,2048]{1,0:T(8,128)(2,1)} %param.12) | copy-start | bytes 25165828
  207.8 10.2 %copy-start.5 = (bf16[2048,512]{1,0:T(8,128)(2,1)S(1)}, bf16[2048,512]{1,0:T(8,128)(2,1)}, u32[]{:S(2)}) copy-start(bf16[2048,512]{1,0:T(8,128)(2,1)} %param.15) | copy-start | bytes 6291460
  391.8 1.3 copy-start.3
  411.6 3.6 copy-start.2
  411.6 3.6 copy-start.6
  415.2 1.6 copy-start.7
  473.1 16.1 %copy-start.4 = (bf16[256,512]{1,0:T(8,128)(2,1)S(1)}, bf16[256,512]{1,0:T(8,128)(2,1)}, u32[]{:S(2)}) copy-start(bf16[256,512]{1,0:T(8,128)(2,1)} %fusion.11.refs_0_) | copy-start | bytes 786436
Sparse Core Ops, SparseCore 0:
  208.0 153.6 reduce-scatter.1

commit v4 on v3

--- a/solution.py
+++ b/solution.py
@@ -112,85 +112,76 @@
     )(*arrays)
 
 
-def spread_kernel(axis, n, across, chunks, x_ref, out_ref, send_sem, recv_sem):
+def spread_kernel(axis, n, x_ref, out_ref, send_a, recv_a, send_b, recv_b):
     me = lax.axis_index(axis)
-    down = n // across
-    z, x = me // across, lax.rem(me, across)
-    root = me == n - 1
+    root = n - 1
     greet(axis, n, me)
-    first = x == across - 1
-    top, below = z == down - 1, z == down - 2
-    inner = jnp.logical_and
-    children = (
-        (
-            (inner(first, z > 0), me - across),
-            (inner(jnp.logical_not(top), x > 0), me - 1),
-            (inner(below, jnp.logical_not(first)), me + across),
-        ),
-        (
-            (inner(top, x > 0), me - 1),
-            (inner(x == 0, z > 0), me - across),
-            (inner(jnp.logical_not(top), jnp.logical_not(first)), me + 1),
-        ),
-    )
-
-    def remote(ref, flow, c, child, to):
-        at = flow * chunks + c
+
+    def parts(j):
+        return (pl.ds(j * n, n), pl.ds(root * n + j, 1))
+
+    tail = pl.ds(root * n + root, 1)
+
+    def remote(src, dst, send, recv, to):
         return pltpu.make_async_remote_copy(
-            src_ref=ref.at[at],
-            dst_ref=out_ref.at[at],
-            send_sem=send_sem.at[child, at],
-            recv_sem=recv_sem.at[at],
+            src_ref=src,
+            dst_ref=dst,
+            send_sem=send,
+            recv_sem=recv,
             device_id={axis: to},
             device_id_type=MESH,
         )
 
-    @pl.when(root)
+    @pl.when(me == root)
     def _():
         copies = []
-        for c in range(chunks):
-            copies.append(remote(out_ref, 0, c, 0, me - across))
-            copies[-1].start()
-            copies.append(remote(out_ref, 1, c, 0, me - 1))
+        for j in range(root):
+            for p, part in enumerate(parts(j)):
+                copies.append(
+                    remote(out_ref.at[part], out_ref.at[part], send_a.at[p, j], recv_a.at[p], j)
+                )
+                copies[-1].start()
+        for j in range(root):
+            copies.append(
+                remote(out_ref.at[tail], out_ref.at[tail], send_a.at[2, j], recv_a.at[2], j)
+            )
             copies[-1].start()
         for copy in copies:
             copy.wait_send()
 
-    @pl.when(jnp.logical_not(root))
+    @pl.when(me != root)
     def _():
-        for c in range(chunks):
-            for flow in range(2):
-                remote(out_ref, flow, c, 0, n - 1).wait_recv()
-                for child, (there, to) in enumerate(children[flow]):
-
-                    @pl.when(there)
-                    def _():
-                        remote(out_ref, flow, c, child, to).start()
-
-        for flow in range(2):
-            for child, (there, to) in enumerate(children[flow]):
-
-                @pl.when(there)
-                def _():
-                    for c in range(chunks):
-                        remote(out_ref, flow, c, child, to).wait_send()
+        copies = []
+        for p, part in enumerate(parts(me)):
+            remote(out_ref.at[part], out_ref.at[part], send_a.at[p, 0], recv_a.at[p], root).wait_recv()
+            for d in range(1, root):
+                to = lax.rem(me + d, root)
+                copies.append(
+                    remote(
+                        out_ref.at[part], out_ref.at[part], send_b.at[p, d], recv_b.at[p, d], to
+                    )
+                )
+                copies[-1].start()
+        remote(out_ref.at[tail], out_ref.at[tail], send_a.at[2, 0], recv_a.at[2], root).wait_recv()
+        for copy in copies:
+            copy.wait()
 
 
 def spread(x, axis, ident):
     n = lax.axis_size(axis)
     rows, width = x.shape
-    across = max(d for d in range(1, n) if n % d == 0 and d * d <= n)
-    chunks = 16
-    grains = x.reshape(2 * chunks, rows // (2 * chunks), width)
+    grains = x.reshape(n * n, rows // (n * n), width)
     out = pl.pallas_call(
-        functools.partial(spread_kernel, axis, n, across, chunks),
+        functools.partial(spread_kernel, axis, n),
         out_shape=jax.ShapeDtypeStruct(grains.shape, x.dtype),
         in_specs=[ANY],
         out_specs=ANY,
         input_output_aliases={0: 0},
         scratch_shapes=[
-            pltpu.SemaphoreType.DMA((3, 2 * chunks)),
-            pltpu.SemaphoreType.DMA((2 * chunks,)),
+            pltpu.SemaphoreType.DMA((3, n)),
+            pltpu.SemaphoreType.DMA((3,)),
+            pltpu.SemaphoreType.DMA((2, n)),
+            pltpu.SemaphoreType.DMA((2, n)),
         ],
         compiler_params=pltpu.CompilerParams(collective_id=ident, has_side_effects=True),
     )(grains)

time: 498 us -> 350 us (0.70)
  Pallas kernels: 426 us -> 278 us
    pallas_call x1, Pallas kernels: 186 us -> 74.8 us  [spread(): pl.pallas_call(functools.partial(spread_kernel, axis, n), out_shape=jax.S...]
    pallas_call x4, Pallas kernels: 140 us -> 102 us  [exchange(): pl.pallas_call(functools.partial(exchange_kernel, axis, n, tuple(modes),...]
  transfers between devices with their start and end apart: 1 -> 1, of which waited for: 0 -> 0; matrix products, arithmetic and copies ran while one was open for 5% -> 8% of each run, Pallas kernels for 32% -> 35%
where the time goes in v4:
time: 350 us; the launch traced here: 349 us
  Pallas kernels  278 us (79%)
  matrix products  35.4 us (10%)
  other arithmetic  16.4 us (5%)
  between operations  13.5 us (4%)
  local copies, waits for them, and re-layouts  5.77 us (2%)
    pallas_call x4, Pallas kernels, exchange(): pl.pallas_call(functools.partial(exchange_kernel, axis, n, tuple(modes),...  102 us
    pallas_call x1, Pallas kernels, spread(): pl.pallas_call(functools.partial(spread_kernel, axis, n), out_shape=jax.S...  74.8 us
    pallas_call x1, Pallas kernels, cross_attention(): pl.pallas_call(functools.partial(cross_kernel, n, hd, 1.0 / math.sqrt(hd)...  42.2 us
    dot_general x7, matrix products, project(): jnp.dot(rows, weight, preferred_element_type=jnp.float32)  35.4 us
    pallas_call x1, Pallas kernels, deal(): pl.pallas_call(functools.partial(deal_kernel, axis, n, heads, hd), out_sh...  32.4 us
    pallas_call x1, Pallas kernels, collect(): pl.pallas_call(functools.partial(collect_kernel, axis, n, heads, hd), out...  11.2 us
    pallas_call x1, Pallas kernels, latent_attention(): pl.pallas_call(functools.partial(latent_kernel, hd, 1.0 / math.sqrt(hd)),...  8.71 us
  transfers between devices with their start and end apart: 1, of which 0 were waited for; matrix products, arithmetic and copies ran while one was open for 8% of the time, Pallas kernels for 35%

profile of v4, /device:TPU:11, one launch (start us, length us, event | category | flops | bytes accessed | tf_op | source)
XLA Modules:
  0.0 348.8 jit_solution(5513511412711807397)
XLA Ops:
  6.5 5.2 %fusion = f32[2048]{0:T(1024)S(1)} fusion(bf16[2048,2048]{1,0:T(8,128)(2,1)} %param.12), kind=kLoop, calls=%fused_computation.2 | loop fusion | flops 12580864 | bytes 8396800 | tf_op jit(solution)/shard_map/reduce_sum | solution.py:20
  12.9 5.8 %convolution_convert_fusion.2 = bf16[2048,512]{1,0:T(8,128)(2,1)} fusion(bf16[2048,512]{1,0:T(8,128)(2,1)S(1)} %copy-done, bf16[2048,2048]{1,0:T(8,128)(2,1)S(1)} %copy-done.1, f32[2048]{0:T(1024)S(1)} %add_rsqrt_fusion), kind=kOutput, calls=%fused_computation.6 | convolution fusion | flops 4308598784 | bytes 12591104 | tf_op jit(solution)/shard_map/dot_general | solution.py:603
  18.7 74.8 %shard_map.118 = bf16[64,32,512]{2,1,0:T(8,128)(2,1)} custom-call(bf16[64,32,512]{2,1,0:T(8,128)(2,1)} %bitcast.39), custom_call_target="tpu_custom_call", output_to_operand_aliasing={{}: (0, {})} | custom-call | tf_op jit(solution)/shard_map/pallas_call | solution.py:174
  93.5 3.3 dynamic-slice_select_fusion
  96.8 10.2 %convolution_convert_fusion.1.k_ref = bf16[2048,512]{1,0:T(8,128)(2,1)} fusion(bf16[2048,512]{1,0:T(8,128)(2,1)} %param.14, bf16[2048,2048]{1,0:T(8,128)(2,1)} %param.12, f32[2048]{0:T(1024)S(1)} %add_rsqrt_fusion), kind=kOutput, calls=%fused_computation.5 | convolution fusion | flops 4308598784 | bytes 12591104 | tf_op jit(solution)/shard_map/dot_general | solution.py:603
  107.1 9.5 %convolution_convert_fusion.v_ref = bf16[2048,512]{1,0:T(8,128)(2,1)} fusion(bf16[2048,512]{1,0:T(8,128)(2,1)S(1)} %copy-done.5, bf16[2048,2048]{1,0:T(8,128)(2,1)} %param.12, f32[2048]{0:T(1024)S(1)} %add_rsqrt_fusion), kind=kOutput, calls=%fused_computation.4 | convolution fusion | flops 4308598784 | bytes 12591104 | tf_op jit(solution)/shard_map/dot_general | solution.py:603
  116.6 42.2 %shard_map.119 = (bf16[2048,512]{1,0:T(8,128)(2,1)}, f32[2048,128]{1,0:T(8,128)}) custom-call(bf16[2048,512]{1,0:T(8,128)(2,1)} %bitcast.40, bf16[2048,512]{1,0:T(8,128)(2,1)} %convolution_convert_fusion.1.k_ref, bf16[2048,512]{1,0:T(8,128)(2,1)} %convolution_convert_fusion.v_ref, s32[4,2048,256]{2,1,0:T(8,128)} %w_ref.3), custom_call_target="tpu_custom_call" | custom-call | flops 34359738368 | bytes 8388608 | tf_op jit(solution)/shard_map/pallas_call | solution.py:464
  158.8 2.2 copy.15
  161.0 59.1 %shard_map.120 = (bf16[8,256,512]{2,1,0:T(8,128)(2,1)}, f32[8,8,256]{2,1,0:T(8,128)}) custom-call(bf16[8,256,512]{2,1,0:T(8,128)(2,1)} %bitcast.38, f32[8,8,256]{2,1,0:T(8,128)} %bitcast.43), custom_call_target="tpu_custom_call" | custom-call | tf_op jit(solution)/shard_map/pallas_call | solution.py:100
  220.1 1.6 copy.16
  221.7 6.2 %shard_map.121.refs_0_ = bf16[256,2048]{1,0:T(8,128)(2,1)} custom-call(bf16[8,256,512]{2,1,0:T(8,128)(2,1)} %get-tuple-element.18.p_ref, f32[256,64]{1,0:T(8,128)} %bitcast.42, bf16[512,2048]{1,0:T(8,128)(2,1)} %w_ref.4), custom_call_target="tpu_custom_call" | custom-call | tf_op jit(solution)/shard_map/pallas_call | solution.py:571
  227.9 14.4 %shard_map.122 = bf16[4,256,512]{2,1,0:T(8,128)(2,1)} custom-call(bf16[256,2048]{1,0:T(8,128)(2,1)} %shard_map.121.refs_0_), custom_call_target="tpu_custom_call" | custom-call | tf_op jit(solution)/shard_map/pallas_call | solution.py:100
  245.2 1.9 fusion.11.refs_0_
  247.2 14.0 %shard_map.123 = bf16[256,2048]{1,0:T(8,128)(2,1)} custom-call(bf16[256,512]{1,0:T(8,128)(2,1)} %fusion.11.refs_0_), custom_call_target="tpu_custom_call" | custom-call | tf_op jit(solution)/shard_map/pallas_call | solution.py:100
  261.2 1.5 fusion.2
  262.8 3.5 %convolution_convert_fusion.6.refs_0_ = bf16[256,512]{1,0:T(8,128)(2,1)} fusion(bf16[2048,512]{1,0:T(8,128)(2,1)} %param.17, bf16[256,2048]{1,0:T(8,128)(2,1)} %shard_map.123, f32[256]{0:T(256)S(1)} %add_rsqrt_fusion.1), kind=kOutput, calls=%fused_computation.17 | convolution fusion | flops 538574848 | bytes 3408896 | tf_op jit(solution)/shard_map/dot_general | solution.py:603
  266.3 1.5 convolution_convert_fusion.5.refs_1_
  267.9 1.5 convolution_convert_fusion.4.refs_2_
  269.4 32.4 %shard_map.124 = (bf16[4,256,128]{2,1,0:T(8,128)(2,1)}, bf16[8,256,128]{2,1,0:T(8,128)(2,1)}, bf16[8,256,128]{2,1,0:T(8,128)(2,1)}) custom-call(bf16[256,512]{1,0:T(8,128)(2,1)} %convolution_convert_fusion.6.refs_0_, bf16[256,512]{1,0:T(8,128)(2,1)} %convolution_convert_fusion.5.refs_1_, bf16[256,512]{1,0:T(8,128)(2,1)} %convolution_convert_fusion.4.refs_2_), custom_call_target="tpu_custom_call" | custom-call | tf_op jit(solution)/shard_map/pallas_call | solution.py:281
  301.7 8.7 %shard_map.125.x_ref = bf16[4,256,128]{2,1,0:T(8,128)(2,1)} custom-call(s32[5]{0:T(128)} %stack.23.at_ref, bf16[4,256,128]{2,1,0:T(8,128)(2,1)} %get-tuple-element.20.q_ref, bf16[8,256,128]{2,1,0:T(8,128)(2,1)} %get-tuple-element.21.k_ref, bf16[8,256,128]{2,1,0:T(8,128)(2,1)} %get-tuple-element.22.v_ref, s32[4,2048,128]{2,1,0:T(8,128)} %w_ref.5), custom_call_target="tpu_custom_call" | custom-call | tf_op jit(solution)/shard_map/pallas_call | solution.py:529
  310.4 11.2 %shard_map.126 = bf16[256,512]{1,0:T(8,128)(2,1)} custom-call(bf16[4,256,128]{2,1,0:T(8,128)(2,1)} %shard_map.125.x_ref), custom_call_target="tpu_custom_call" | custom-call | tf_op jit(solution)/shard_map/pallas_call | solution.py:353
  321.7 3.4 convolution_convert_fusion.3.refs_0_
  325.0 14.6 %shard_map.127 = bf16[4,256,512]{2,1,0:T(8,128)(2,1)} custom-call(bf16[256,2048]{1,0:T(8,128)(2,1)} %convolution_convert_fusion.3.refs_0_), custom_call_target="tpu_custom_call" | custom-call | tf_op jit(solution)/shard_map/pallas_call | solution.py:100
  339.7 1.4 convert_reduce_fusion
  (26 shorter events, 5.0 us)
Async XLA Ops:
  6.5 5.3 %copy-start = (bf16[2048,512]{1,0:T(8,128)(2,1)S(1)}, bf16[2048,512]{1,0:T(8,128)(2,1)}, u32[]{:S(2)}) copy-start(bf16[2048,512]{1,0:T(8,128)(2,1)} %param.13) | copy-start | bytes 6291460
  6.5 238.7 %reduce-scatter.2.cloned.1.call-start = ((), (), s32[]{:S(2)}) async-start(), calls=%async_computation.1 | async-start | bytes 2359296 | tf_op jit(solution)/shard_map/reduce_scatter | solution.py:613
  6.5 6.4 %copy-start.1 = (bf16[2048,2048]{1,0:T(8,128)(2,1)S(1)}, bf16[2048,2048]{1,0:T(8,128)(2,1)}, u32[]{:S(2)}) copy-start(bf16[2048,2048]{1,0:T(8,128)(2,1)} %param.12) | copy-start | bytes 25165828
  96.8 10.2 %copy-start.5 = (bf16[2048,512]{1,0:T(8,128)(2,1)S(1)}, bf16[2048,512]{1,0:T(8,128)(2,1)}, u32[]{:S(2)}) copy-start(bf16[2048,512]{1,0:T(8,128)(2,1)} %param.15) | copy-start | bytes 6291460
  243.0 1.3 copy-start.3
  262.7 3.6 %copy-start.2 = (bf16[256,2048]{1,0:T(8,128)(2,1)S(1)}, bf16[256,2048]{1,0:T(8,128)(2,1)}, u32[]{:S(2)}) copy-start(bf16[256,2048]{1,0:T(8,128)(2,1)} %shard_map.123) | copy-start | bytes 3145732
  262.7 3.6 %copy-start.6 = (bf16[2048,512]{1,0:T(8,128)(2,1)S(1)}, bf16[2048,512]{1,0:T(8,128)(2,1)}, u32[]{:S(2)}) copy-start(bf16[2048,512]{1,0:T(8,128)(2,1)} %param.18) | copy-start | bytes 6291460
  266.3 1.6 copy-start.7
  325.0 16.1 %copy-start.4 = (bf16[256,512]{1,0:T(8,128)(2,1)S(1)}, bf16[256,512]{1,0:T(8,128)(2,1)}, u32[]{:S(2)}) copy-start(bf16[256,512]{1,0:T(8,128)(2,1)} %fusion.11.refs_0_) | copy-start | bytes 786436
Sparse Core Ops, SparseCore 0:
  96.9 66.6 reduce-scatter.1
